TPU v7x, 128 devices: a whole 4x4x4 slice. The times are simulated.
128 devices in a mesh: head: 4 (over z), seq: 32 (over y, x, core).
Axes of the slice: x: 4, y: 4, z: 4, core: 2. Of those that a mesh axis runs over, the one named last changes fastest.
Arguments:
- queries: bfloat16 [16384, 6144], P('seq', 'head'), may hold values from -60 to 60
- keys: bfloat16 [16384, 6144], P('seq', 'head'), may hold values from -6 to 6
- values: bfloat16 [16384, 6144], P('seq', 'head'), may hold values from -6 to 6
- cluster_ids: int32 [4, 16384, 1], P('head', 'seq'), may hold values from 0 to 255, as said below
- w_out: bfloat16 [6144, 6144], P('head'), may hold values from -0.078125 to 0.078125
Outputs:
- projected: bfloat16 [16384, 6144], P('seq', 'head')
Inputs may be any that keep to these rules, and one draw needn't show every extreme that they name: `cluster_ids`: cluster c is owned by index c // (256 / 32) of seq. Among the 512 tokens of one index of seq, in one head group, at most 4 name the same cluster and at most 24 name clusters of the same owner; both bounds are reached in every such block.
All inputs are finite; a program needn't handle non-finite values.
Results may differ from a plain program's by a relative error of at most 0.009.
Values may be sent and summed in bfloat16 or wider, within the bound.
A program may use at most 128 MiB of HBM per device.

v0:
```python
import math

import jax
import jax.numpy as jnp
from jax import lax
from jax.sharding import PartitionSpec as P

HD = 128
NCLUST = 256
CAP = 4
OWNER_CAP = 24
NSPLIT = 2


def attend(queries, keys, values, counts):
    batch, rows_all, features = queries.shape
    heads_here = features // HD
    capacity = rows_all // counts.shape[1]
    head_shape = (batch, rows_all, heads_here, HD)
    scores = jnp.einsum(
        "bqhd,bkhd->bhqk",
        queries.reshape(head_shape),
        keys.reshape(head_shape),
        preferred_element_type=jnp.float32,
    ) * (1.0 / math.sqrt(HD))
    key_order = jnp.arange(rows_all, dtype=jnp.int32)
    filled = jnp.repeat(counts.astype(jnp.float32), capacity, axis=1)
    present = (key_order % capacity).astype(jnp.float32)[None, :] < filled
    causal = key_order[None, :] <= key_order[:, None]
    diagonal_on = key_order[None, :] == key_order[:, None]
    allowed = present[:, None, None, :] & causal[None, None] | diagonal_on[None, None]
    scores = jnp.where(allowed, scores, -1e30)
    row_max = jnp.max(scores, axis=-1, keepdims=True)
    exp_scores = jnp.exp(scores - row_max)
    totals = jnp.sum(exp_scores, axis=-1)
    weights = exp_scores.astype(jnp.bfloat16)
    attended = jnp.einsum(
        "bhqk,bkhd->bqhd", weights, values.reshape(head_shape), preferred_element_type=jnp.float32
    )
    attended = attended / jnp.transpose(totals, (0, 2, 1))[..., None]
    return attended.astype(jnp.bfloat16).reshape(batch, rows_all, features)


def attend_heads(queries, keys, values, counts):
    heads_here, batch, rows_all, _ = queries.shape
    capacity = rows_all // counts.shape[1]
    scores = jnp.einsum(
        "hbqd,hbkd->hbqk", queries, keys, preferred_element_type=jnp.float32
    ) * (1.0 / math.sqrt(HD))
    key_order = jnp.arange(rows_all, dtype=jnp.int32)
    filled = jnp.repeat(counts.astype(jnp.float32), capacity, axis=1)
    present = (key_order % capacity).astype(jnp.float32)[None, :] < filled
    causal = key_order[None, :] <= key_order[:, None]
    diagonal_on = key_order[None, :] == key_order[:, None]
    allowed = present[:, None, :] & causal[None] | diagonal_on[None]
    scores = jnp.where(allowed[None], scores, -1e30)
    row_max = jnp.max(scores, axis=-1, keepdims=True)
    exp_scores = jnp.exp(scores - row_max)
    totals = jnp.sum(exp_scores, axis=-1, keepdims=True)
    weights = exp_scores.astype(jnp.bfloat16)
    attended = jnp.einsum("hbqk,hbkd->hbqd", weights, values, preferred_element_type=jnp.float32)
    attended = attended / totals
    return attended.astype(jnp.bfloat16).reshape(heads_here, batch * rows_all, HD)


def one_hot(index, size):
    return (index[:, None] == jnp.arange(size, dtype=jnp.int32)[None, :]).astype(jnp.bfloat16)


def permute(selector, block):
    return jnp.dot(selector, block, preferred_element_type=jnp.float32).astype(jnp.bfloat16)


def body(queries, keys, values, cluster_ids, w_out):
    cluster = cluster_ids[0, :, 0]
    tokens = cluster.shape[0]
    seq_count = lax.axis_size("seq")
    cl_dev = NCLUST // seq_count
    features = queries.shape[1]
    heads_here = features // HD
    split = NSPLIT if heads_here % NSPLIT == 0 else 1
    part = features // split
    rows = OWNER_CAP
    slots = seq_count * rows
    bucket_rows = cl_dev * seq_count * CAP
    owner = cluster // cl_dev
    position = jnp.arange(tokens, dtype=jnp.int32)

    order_key = cluster * tokens + position
    same_owner = owner[:, None] == owner[None, :]
    before = order_key[None, :] < order_key[:, None]
    rank = jnp.sum((same_owner & before).astype(jnp.int32), axis=1)
    dest = owner * rows + rank
    to_token = one_hot(dest, slots)
    to_slot = to_token.T

    counts = jnp.sum(
        (cluster[:, None] == jnp.arange(NCLUST, dtype=jnp.int32)[None, :]).astype(jnp.int32),
        axis=0,
    ).reshape(seq_count, cl_dev)
    count_in = lax.all_to_all(counts, "seq", 0, 0, tiled=True)

    ends = jnp.cumsum(count_in, axis=1)
    j = jnp.arange(rows, dtype=jnp.int32)
    c_of = jnp.sum((ends[:, None, :] <= j[None, :, None]).astype(jnp.int32), axis=2)
    row_cluster = c_of.reshape(slots)
    valid = row_cluster < cl_dev
    flat = jnp.arange(slots, dtype=jnp.int32)
    allowed = (
        (row_cluster[:, None] == row_cluster[None, :])
        & valid[None, :]
        & (flat[None, :] <= flat[:, None])
    ) | (flat[None, :] == flat[:, None])

    partial_value = None
    for k in range(split):
        cols = slice(k * part, (k + 1) * part)
        packed = jnp.concatenate([queries[:, cols], keys[:, cols], values[:, cols]], axis=1)
        outgoing = permute(to_slot, packed).reshape(seq_count, rows, 3 * part)
        incoming = lax.all_to_all(outgoing, "seq", 0, 0, tiled=True).reshape(slots, 3 * part)
        heads_part = part // HD
        head_shape = (slots, heads_part, HD)
        scores = jnp.einsum(
            "qhd,khd->hqk",
            incoming[:, :part].reshape(head_shape),
            incoming[:, part : 2 * part].reshape(head_shape),
            preferred_element_type=jnp.float32,
        ) * (1.0 / math.sqrt(HD))
        scores = jnp.where(allowed[None], scores, -1e30)
        row_max = jnp.max(scores, axis=-1, keepdims=True)
        exp_scores = jnp.exp(scores - row_max)
        totals = jnp.sum(exp_scores, axis=-1)
        weights = exp_scores.astype(jnp.bfloat16)
        attended = jnp.einsum(
            "hqk,khd->qhd",
            weights,
            incoming[:, 2 * part :].reshape(head_shape),
            preferred_element_type=jnp.float32,
        )
        attended = attended / totals.T[:, :, None]
        back = attended.astype(jnp.bfloat16).reshape(seq_count, rows, part)
        returned = lax.all_to_all(back, "seq", 0, 0, tiled=True)
        own_rows = permute(to_token, returned.reshape(slots, part))
        term = jnp.dot(own_rows, w_out[cols], preferred_element_type=jnp.float32)
        partial_value = term if partial_value is None else partial_value + term
    summed = lax.psum_scatter(
        partial_value.astype(jnp.bfloat16), "head", scatter_dimension=1, tiled=True
    )
    return summed


def solution(mesh):
    return jax.shard_map(
        body,
        mesh=mesh,
        in_specs=(
            P("seq", "head"),
            P("seq", "head"),
            P("seq", "head"),
            P("head", "seq", None),
            P("head", None),
        ),
        out_specs=P("seq", "head"),
        check_vma=False,
    )
```

profile of v0, /device:TPU:1, one launch (start us, length us, event | category | flops | bytes accessed | tf_op | source)
XLA Modules:
  0.0 303.4 jit_solution(8494504882379905042)
XLA Ops:
  8.2 8.6 %all-to-all-start.1 = ((s32[32,1,8]{2,1,0:T(1,128)}), s32[32,1,8]{2,1,0:T(1,128)S(1)}, u32[]{:S(2)}, u32[]{:S(2)}) async-start(s32[32,1,8]{2,1,0:T(1,128)} %bitcast.4), calls=%async_computation.1 | async-start | bytes 32768 | tf_op jit(solution)/shard_map/all_to_all | solution.py:101
  17.9 2.4 fusion.58
  21.6 4.0 %convolution_convert_fusion.1 = bf16[768,2304]{1,0:T(8,128)(2,1)} fusion(bf16[512,768]{1,0:T(8,128)(2,1)S(1)} %get-tuple-element.17, bf16[512,768]{1,0:T(8,128)(2,1)S(1)} %get-tuple-element.25, bf16[512,768]{1,0:T(8,128)(2,1)S(1)} %get-tuple-element.13, s32[512]{0:T(512)S(1)} %multiply_add_fusion), kind=kOutput, calls=%fused_computation.20 | convolution fusion | flops 1821179904 | bytes 5900288 | tf_op jit(solution)/shard_map/dot_general | solution.py:71
  26.2 7.4 %all-to-all-start = ((bf16[32,24,2304]{2,1,0:T(8,128)(2,1)}), bf16[32,24,2304]{2,1,0:T(8,128)(2,1)S(1)}, u32[]{:S(2)}, u32[]{:S(2)}) async-start(bf16[32,24,2304]{2,1,0:T(8,128)(2,1)} %bitcast.38), calls=%async_computation | async-start | bytes 7077888 | tf_op jit(solution)/shard_map/all_to_all | solution.py:120
  33.6 5.5 %convolution_convert_fusion = bf16[768,2304]{1,0:T(8,128)(2,1)} fusion(bf16[512,768]{1,0:T(8,128)(2,1)} %get-tuple-element.18, bf16[512,768]{1,0:T(8,128)(2,1)} %get-tuple-element.24, bf16[512,768]{1,0:T(8,128)(2,1)} %get-tuple-element.14, s32[512]{0:T(512)} %copy-done.11), kind=kOutput, calls=%fused_computation.19 | convolution fusion | flops 1821179904 | bytes 5900288 | tf_op jit(solution)/shard_map/dot_general | solution.py:71
  39.1 38.5 %all-to-all-done = bf16[32,24,2304]{2,1,0:T(8,128)(2,1)S(1)} async-done(((bf16[32,24,2304]{2,1,0:T(8,128)(2,1)}), bf16[32,24,2304]{2,1,0:T(8,128)(2,1)S(1)}, u32[]{:S(2)}, u32[]{:S(2)}) %all-to-all-start) | async-done | bytes 3538976 | tf_op jit(solution)/shard_map/all_to_all | solution.py:120
  77.5 1.8 copy-done
  79.3 6.5 %all-to-all-start.3 = ((bf16[32,24,2304]{2,1,0:T(8,128)(2,1)}), bf16[32,24,2304]{2,1,0:T(8,128)(2,1)S(1)}, u32[]{:S(2)}, u32[]{:S(2)}) async-start(bf16[32,24,2304]{2,1,0:T(8,128)(2,1)} %bitcast.37), calls=%async_computation.3 | async-start | bytes 7077888 | tf_op jit(solution)/shard_map/all_to_all | solution.py:120
  90.9 3.9 %fusion.54 = (bf16[768,768]{1,0:T(8,128)(2,1)}, bf16[768,768]{1,0:T(8,128)(2,1)}, bf16[768,768]{1,0:T(8,128)(2,1)}) fusion(bf16[768,2304]{1,0:T(8,128)(2,1)} %bitcast.34), kind=kLoop, calls=%fused_computation.69 | loop fusion | bytes 7077888 | tf_op jit(solution)/shard_map/slice | solution.py:137
  94.7 2.4 copy.49
  97.1 2.4 copy.54
  99.5 2.4 copy.53
  101.9 27.6 %all-to-all-done.3 = bf16[32,24,2304]{2,1,0:T(8,128)(2,1)S(1)} async-done(((bf16[32,24,2304]{2,1,0:T(8,128)(2,1)}), bf16[32,24,2304]{2,1,0:T(8,128)(2,1)S(1)}, u32[]{:S(2)}, u32[]{:S(2)}) %all-to-all-start.3) | async-done | bytes 3538976 | tf_op jit(solution)/shard_map/all_to_all | solution.py:120
  129.5 1.9 fusion.55
  131.4 2.4 copy.61
  133.8 2.5 copy.60
  136.3 2.4 copy.59
  138.7 2.7 fusion
  141.4 10.7 %fusion.2 = (f32[6,768]{1,0:T(8,128)S(1)}, f32[6,768]{1,0:T(8,128)S(1)}, f32[6,768,768]{1,2,0:T(8,128)}) fusion(f32[6,768,768]{1,2,0:T(8,128)S(1)} %get-tuple-element.22, f32[6,768]{1,0:T(8,128)S(1)} %get-tuple-element.21, pred[768,768]{0,1:T(8,128)(4,1)S(1)} %copy-done.2, bf16[768,6,128]{0,2,1:T(8,128)(2,1)} %bitcast.41, bf16[768,6,128]{0,2,1:T(8,128)(2,1)S(1)} %bitcast.40), kind=kOutput, calls=%fused_computation.7 | convolution fusion | flops 930733056 | bytes 31315968 | tf_op jit(solution)/shard_map/qhd,khd->hqk/dot_general | solution.py:123
  152.1 8.1 %fusion.4 = f32[6,768]{1,0:T(8,128)S(1)} fusion(f32[6,768,768]{1,2,0:T(8,128)} %get-tuple-element.23, f32[6,768]{1,0:T(8,128)S(1)} %get-tuple-element.6, pred[768,768]{0,1:T(8,128)(4,1)S(1)} %copy-done.2), kind=kLoop, calls=%fused_computation.9 | loop fusion | flops 14151168 | bytes 14782464 | tf_op jit(solution)/shard_map/reduce_sum | solution.py:132
  160.1 9.1 %fusion.28 = bf16[768,6,128]{0,2,1:T(8,128)(2,1)S(1)} fusion(bf16[768,6,128]{0,2,1:T(8,128)(2,1)S(1)} %bitcast.42, f32[6,768,768]{1,2,0:T(8,128)} %get-tuple-element.23, f32[6,768]{1,0:T(8,128)S(1)} %get-tuple-element.6, pred[768,768]{0,1:T(8,128)(4,1)S(1)} %copy-done.2, f32[768,6]{0,1:T(8,128)S(1)} %bitcast.45), kind=kOutput, calls=%fused_computation.32 | convolution fusion | flops 921305088 | bytes 17141760 | tf_op jit(solution)/shard_map/hqk,khd->qhd/dot_general | solution.py:134
  170.4 2.2 reshape.233
  172.6 7.3 %all-to-all-start.4 = ((bf16[32,24,768]{2,1,0:T(8,128)(2,1)}), bf16[32,24,768]{2,1,0:T(8,128)(2,1)}, u32[]{:S(2)}, u32[]{:S(2)}) async-start(bf16[32,24,768]{2,1,0:T(8,128)(2,1)} %reshape.233), calls=%async_computation.4 | async-start | bytes 2359296 | tf_op jit(solution)/shard_map/all_to_all | solution.py:142
  179.9 10.0 %fusion.29 = bf16[768,6,128]{0,2,1:T(8,128)(2,1)} fusion(bf16[768,6,128]{0,2,1:T(8,128)(2,1)S(1)} %bitcast.39, f32[6,768,768]{1,2,0:T(8,128)} %copy-done.1, f32[6,768]{1,0:T(8,128)S(1)} %get-tuple-element.21, pred[768,768]{0,1:T(8,128)(4,1)S(1)} %copy-done.2, f32[768,6]{0,1:T(8,128)S(1)} %bitcast.48), kind=kOutput, calls=%fused_computation.34 | convolution fusion | flops 921305088 | bytes 17141760 | tf_op jit(solution)/shard_map/hqk,khd->qhd/dot_general | solution.py:134
  190.0 2.1 copy.58
  192.0 2.2 reshape.226
  194.3 4.4 %all-to-all-done.4 = bf16[32,24,768]{2,1,0:T(8,128)(2,1)} async-done(((bf16[32,24,768]{2,1,0:T(8,128)(2,1)}), bf16[32,24,768]{2,1,0:T(8,128)(2,1)}, u32[]{:S(2)}, u32[]{:S(2)}) %all-to-all-start.4) | async-done | bytes 1179680 | tf_op jit(solution)/shard_map/all_to_all | solution.py:142
  198.6 4.0 %all-to-all-start.2 = ((bf16[32,24,768]{2,1,0:T(8,128)(2,1)}), bf16[32,24,768]{2,1,0:T(8,128)(2,1)S(1)}, u32[]{:S(2)}, u32[]{:S(2)}) async-start(bf16[32,24,768]{2,1,0:T(8,128)(2,1)} %reshape.226), calls=%async_computation.2 | async-start | bytes 2359296 | tf_op jit(solution)/shard_map/all_to_all | solution.py:142
  202.7 11.9 %fusion.6 = f32[512,6144]{1,0:T(8,128)} fusion(bf16[1536,6144]{1,0:T(8,128)(2,1)} %param.9, bf16[768,768]{1,0:T(8,128)(2,1)} %bitcast.18, s32[512]{0:T(512)S(1)} %copy-done.12), kind=kOutput, calls=%fused_computation.11 | convolution fusion | flops 5436604416 | bytes 23201792 | tf_op jit(solution)/shard_map/dot_general | solution.py:144
  214.6 6.7 %all-to-all-done.2 = bf16[32,24,768]{2,1,0:T(8,128)(2,1)S(1)} async-done(((bf16[32,24,768]{2,1,0:T(8,128)(2,1)}), bf16[32,24,768]{2,1,0:T(8,128)(2,1)S(1)}, u32[]{:S(2)}, u32[]{:S(2)}) %all-to-all-start.2) | async-done | bytes 1179680 | tf_op jit(solution)/shard_map/all_to_all | solution.py:142
  221.3 12.6 %add_convert_fusion = bf16[512,6144]{1,0:T(8,128)(2,1)} fusion(f32[512,6144]{1,0:T(8,128)} %fusion.6, bf16[1536,6144]{1,0:T(8,128)(2,1)} %param.9, bf16[768,768]{1,0:T(8,128)(2,1)S(1)} %bitcast.43, s32[512]{0:T(512)S(1)} %copy-done.12), kind=kOutput, calls=%fused_computation.4 | convolution fusion | flops 5442895872 | bytes 29493248 | tf_op jit(solution)/shard_map/dot_general | solution.py:144
  233.9 62.7 %reduce-scatter.2.cloned.1.call-done = bf16[512,1536]{1,0:T(8,128)(2,1)} async-done(((bf16[512,6144]{1,0:T(8,128)(2,1)}), bf16[512,1536]{1,0:T(8,128)(2,1)}) %reduce-scatter.2.cloned.1.call-update) | async-done | bytes 1572880 | tf_op jit(solution)/shard_map/reduce_scatter | solution.py:146
  (42 shorter events, 11.0 us)
Async XLA Ops:
  6.5 13.7 %copy-start.6 = (bf16[512,1536]{1,0:T(8,128)(2,1)S(1)}, bf16[512,1536]{1,0:T(8,128)(2,1)}, u32[]{:S(2)}) copy-start(bf16[512,1536]{1,0:T(8,128)(2,1)} %param.6) | copy-start | bytes 4718596
  6.5 13.7 %copy-start.5 = (bf16[512,1536]{1,0:T(8,128)(2,1)S(1)}, bf16[512,1536]{1,0:T(8,128)(2,1)}, u32[]{:S(2)}) copy-start(bf16[512,1536]{1,0:T(8,128)(2,1)} %param.5) | copy-start | bytes 4718596
  8.2 17.4 %all-to-all-start.1 = ((s32[32,1,8]{2,1,0:T(1,128)}), s32[32,1,8]{2,1,0:T(1,128)S(1)}, u32[]{:S(2)}, u32[]{:S(2)}) async-start(s32[32,1,8]{2,1,0:T(1,128)} %bitcast.4), calls=%async_computation.1 | async-start | bytes 32768 | tf_op jit(solution)/shard_map/all_to_all | solution.py:101
  17.8 3.8 %copy-start.11 = (s32[512]{0:T(512)}, s32[512]{0:T(512)S(1)}, u32[]{:S(2)}) copy-start(s32[512]{0:T(512)S(1)} %multiply_add_fusion) | copy-start | bytes 6148
  25.6 0.6 copy-start.10
  26.2 51.3 %all-to-all-start = ((bf16[32,24,2304]{2,1,0:T(8,128)(2,1)}), bf16[32,24,2304]{2,1,0:T(8,128)(2,1)S(1)}, u32[]{:S(2)}, u32[]{:S(2)}) async-start(bf16[32,24,2304]{2,1,0:T(8,128)(2,1)} %bitcast.38), calls=%async_computation | async-start | bytes 7077888 | tf_op jit(solution)/shard_map/all_to_all | solution.py:120
  77.5 1.8 copy-start
  79.3 50.2 %all-to-all-start.3 = ((bf16[32,24,2304]{2,1,0:T(8,128)(2,1)}), bf16[32,24,2304]{2,1,0:T(8,128)(2,1)S(1)}, u32[]{:S(2)}, u32[]{:S(2)}) async-start(bf16[32,24,2304]{2,1,0:T(8,128)(2,1)} %bitcast.37), calls=%async_computation.3 | async-start | bytes 7077888 | tf_op jit(solution)/shard_map/all_to_all | solution.py:120
  133.7 4.9 %copy-start.2 = (pred[768,768]{0,1:T(8,128)(4,1)S(1)}, pred[768,768]{0,1:T(8,128)(4,1)}, u32[]{:S(2)}) copy-start(pred[768,768]{0,1:T(8,128)(4,1)} %fusion.31) | copy-start | bytes 1769476
  133.8 4.9 %copy-start.3 = (bf16[768,768]{0,1:T(8,128)(2,1)S(1)}, bf16[768,768]{0,1:T(8,128)(2,1)}, u32[]{:S(2)}) copy-start(bf16[768,768]{0,1:T(8,128)(2,1)} %copy.54) | copy-start | bytes 3538948
  133.8 4.9 %copy-start.4 = (bf16[768,768]{0,1:T(8,128)(2,1)S(1)}, bf16[768,768]{0,1:T(8,128)(2,1)}, u32[]{:S(2)}) copy-start(bf16[768,768]{0,1:T(8,128)(2,1)} %copy.53) | copy-start | bytes 3538948
  138.7 2.7 copy-start.8
  141.4 10.7 %copy-start.1 = (f32[6,768,768]{1,2,0:T(8,128)}, f32[6,768,768]{1,2,0:T(8,128)S(1)}, u32[]{:S(2)}) copy-start(f32[6,768,768]{1,2,0:T(8,128)S(1)} %get-tuple-element.22) | copy-start | bytes 42467332
  152.1 8.1 %copy-start.9 = (bf16[768,768]{0,1:T(8,128)(2,1)S(1)}, bf16[768,768]{0,1:T(8,128)(2,1)}, u32[]{:S(2)}) copy-start(bf16[768,768]{0,1:T(8,128)(2,1)} %copy.59) | copy-start | bytes 3538948
  170.4 9.6 %copy-start.7 = (bf16[768,768]{0,1:T(8,128)(2,1)S(1)}, bf16[768,768]{0,1:T(8,128)(2,1)}, u32[]{:S(2)}) copy-start(bf16[768,768]{0,1:T(8,128)(2,1)} %copy.49) | copy-start | bytes 3538948
  172.6 26.0 %all-to-all-start.4 = ((bf16[32,24,768]{2,1,0:T(8,128)(2,1)}), bf16[32,24,768]{2,1,0:T(8,128)(2,1)}, u32[]{:S(2)}, u32[]{:S(2)}) async-start(bf16[32,24,768]{2,1,0:T(8,128)(2,1)} %reshape.233), calls=%async_computation.4 | async-start | bytes 2359296 | tf_op jit(solution)/shard_map/all_to_all | solution.py:142
  192.0 10.6 %copy-start.12 = (s32[512]{0:T(512)S(1)}, s32[512]{0:T(512)}, u32[]{:S(2)}) copy-start(s32[512]{0:T(512)} %copy-done.11) | copy-start | bytes 6148
  198.6 22.6 %all-to-all-start.2 = ((bf16[32,24,768]{2,1,0:T(8,128)(2,1)}), bf16[32,24,768]{2,1,0:T(8,128)(2,1)S(1)}, u32[]{:S(2)}, u32[]{:S(2)}) async-start(bf16[32,24,768]{2,1,0:T(8,128)(2,1)} %reshape.226), calls=%async_computation.2 | async-start | bytes 2359296 | tf_op jit(solution)/shard_map/all_to_all | solution.py:142
  202.6 94.0 %reduce-scatter.2.cloned.1.call-start = ((), (), s32[]{:S(2)}) async-start(), calls=%async_computation.6 | async-start | bytes 7864320 | tf_op jit(solution)/shard_map/reduce_scatter | solution.py:146
Sparse Core Ops, SparseCore 0:
  234.1 62.4 reduce-scatter.1
where the time goes:
time: 304 us; the launch traced here: 303 us
  waiting for transfers between devices  140 us (46%)
  matrix products  66.4 us (22%)
  local copies, waits for them, and re-layouts  36.9 us (12%)
  starting transfers between devices  33.8 us (11%)
  between operations  13.6 us (4%)
  other arithmetic  13 us (4%)
    all_to_all x2, waiting for transfers between devices, body(): lax.all_to_all(outgoing, 'seq', 0, 0, tiled=True).reshape(slots, 3 * part)  66.1 us
    reduce_scatter x1, waiting for transfers between devices, body(): lax.psum_scatter(partial_value.astype(jnp.bfloat16), 'head', scatter_dime...  62.7 us
    dot_general x2, matrix products, body(): term = jnp.dot(own_rows, w_out[cols], preferred_element_type=jnp.float32)  24.6 us
    dot_general x2, matrix products, body(): jnp.einsum('hqk,khd->qhd', weights, incoming[:, 2 * part:].reshape(head_s...  19.1 us
    all_to_all x2, starting transfers between devices, body(): lax.all_to_all(outgoing, 'seq', 0, 0, tiled=True).reshape(slots, 3 * part)  13.9 us
    dot_general x2, matrix products, body(): jnp.einsum('qhd,khd->hqk', incoming[:, :part].reshape(head_shape), incomi...  13.3 us
    all_to_all x2, starting transfers between devices, body(): returned = lax.all_to_all(back, 'seq', 0, 0, tiled=True)  11.3 us
    all_to_all x2, waiting for transfers between devices, body(): returned = lax.all_to_all(back, 'seq', 0, 0, tiled=True)  11 us
  transfers between devices with their start and end apart: 6, of which 5 were waited for; matrix products, arithmetic and copies ran while one was open for 19% of the time, Pallas kernels for 0%

commit v1 on v0

--- a/solution.py
+++ b/solution.py
@@ -118,6 +118,12 @@
         packed = jnp.concatenate([queries[:, cols], keys[:, cols], values[:, cols]], axis=1)
         outgoing = permute(to_slot, packed).reshape(seq_count, rows, 3 * part)
         incoming = lax.all_to_all(outgoing, "seq", 0, 0, tiled=True).reshape(slots, 3 * part)
+        if k > 0:
+            incoming, back = lax.optimization_barrier((incoming, back))
+            returned = lax.all_to_all(back, "seq", 0, 0, tiled=True)
+            own_rows = permute(to_token, returned.reshape(slots, part))
+            term = jnp.dot(own_rows, w_out[prev_cols], preferred_element_type=jnp.float32)
+            partial_value = term if partial_value is None else partial_value + term
         heads_part = part // HD
         head_shape = (slots, heads_part, HD)
         scores = jnp.einsum(
@@ -139,10 +145,11 @@
         )
         attended = attended / totals.T[:, :, None]
         back = attended.astype(jnp.bfloat16).reshape(seq_count, rows, part)
-        returned = lax.all_to_all(back, "seq", 0, 0, tiled=True)
-        own_rows = permute(to_token, returned.reshape(slots, part))
-        term = jnp.dot(own_rows, w_out[cols], preferred_element_type=jnp.float32)
-        partial_value = term if partial_value is None else partial_value + term
+        prev_cols = cols
+    returned = lax.all_to_all(back, "seq", 0, 0, tiled=True)
+    own_rows = permute(to_token, returned.reshape(slots, part))
+    term = jnp.dot(own_rows, w_out[prev_cols], preferred_element_type=jnp.float32)
+    partial_value = term if partial_value is None else partial_value + term
     summed = lax.psum_scatter(
         partial_value.astype(jnp.bfloat16), "head", scatter_dimension=1, tiled=True
     )

time: 304 us -> 296 us (0.974)
  waiting for transfers between devices: 140 us -> 112 us
  blocking collectives: 0 us -> 25.4 us
  other arithmetic: 13 us -> 20.2 us
  starting transfers between devices: 33.8 us -> 27.3 us
  local copies, waits for them, and re-layouts: 36.9 us -> 31.3 us
    all_to_all x0 -> x1, blocking collectives: none -> 25.4 us  [body(): returned = lax.all_to_all(back, 'seq', 0, 0, tiled=True)]
    all_to_all x2, waiting for transfers between devices: 66.1 us -> 42.8 us  [body(): lax.all_to_all(outgoing, 'seq', 0, 0, tiled=True).reshape(slots, 3 * part)]
    reduce_sum x1 -> x2, other arithmetic: 8.08 us -> 16.1 us  [body(): totals = jnp.sum(exp_scores, axis=-1)]
    all_to_all x2 -> x1, starting transfers between devices: 11.3 us -> 4.13 us  [body(): returned = lax.all_to_all(back, 'seq', 0, 0, tiled=True)]
    all_to_all x2 -> x1, waiting for transfers between devices: 11 us -> 6.69 us  [body(): returned = lax.all_to_all(back, 'seq', 0, 0, tiled=True)]
    slice x3 -> x2, local copies, waits for them, and re-layouts: 8.61 us -> 4.75 us  [body(): incoming[:, 2 * part:].reshape(head_shape)]
    slice x3 -> x4, local copies, waits for them, and re-layouts: 6.62 us -> 10.4 us  [body(): incoming[:, part:2 * part].reshape(head_shape)]
    slice x2, local copies, waits for them, and re-layouts: 4.96 us -> 1.27 us  [body(): incoming[:, :part].reshape(head_shape)]
  transfers between devices with their start and end apart: 6 -> 5, of which waited for: 5 -> 4; matrix products, arithmetic and copies ran while one was open for 19% -> 22% of each run, Pallas kernels for 0% -> 0%
where the time goes in v1:
time: 296 us; the launch traced here: 295 us
  waiting for transfers between devices  112 us (38%)
  matrix products  64.8 us (22%)
  local copies, waits for them, and re-layouts  31.3 us (11%)
  starting transfers between devices  27.3 us (9%)
  blocking collectives  25.4 us (9%)
  other arithmetic  20.2 us (7%)
  between operations  13.6 us (5%)
    reduce_scatter x1, waiting for transfers between devices, body(): lax.psum_scatter(partial_value.astype(jnp.bfloat16), 'head', scatter_dime...  62.6 us
    all_to_all x2, waiting for transfers between devices, body(): lax.all_to_all(outgoing, 'seq', 0, 0, tiled=True).reshape(slots, 3 * part)  42.8 us
    all_to_all x1, blocking collectives, body(): returned = lax.all_to_all(back, 'seq', 0, 0, tiled=True)  25.4 us
    dot_general x2, matrix products, body(): jnp.dot(own_rows, w_out[prev_cols], preferred_element_type=jnp.float32)  24.5 us
    dot_general x2, matrix products, body(): jnp.einsum('hqk,khd->qhd', weights, incoming[:, 2 * part:].reshape(head_s...  18.1 us
    reduce_sum x2, other arithmetic, body(): totals = jnp.sum(exp_scores, axis=-1)  16.1 us
    all_to_all x2, starting transfers between devices, body(): lax.all_to_all(outgoing, 'seq', 0, 0, tiled=True).reshape(slots, 3 * part)  14.6 us
    dot_general x2, matrix products, body(): jnp.einsum('qhd,khd->hqk', incoming[:, :part].reshape(head_shape), incomi...  12.8 us
  transfers between devices with their start and end apart: 5, of which 4 were waited for; matrix products, arithmetic and copies ran while one was open for 22% of the time, Pallas kernels for 0%

profile of v1, /device:TPU:1, one launch (start us, length us, event | category | flops | bytes accessed | tf_op | source)
XLA Modules:
  0.0 294.7 jit_solution(8597075111284215327)
XLA Ops:
  8.2 8.6 %all-to-all-start.2 = ((s32[32,1,8]{2,1,0:T(1,128)}), s32[32,1,8]{2,1,0:T(1,128)S(1)}, u32[]{:S(2)}, u32[]{:S(2)}) async-start(s32[32,1,8]{2,1,0:T(1,128)} %bitcast.6), calls=%async_computation.2 | async-start | bytes 32768 | tf_op jit(solution)/shard_map/all_to_all | solution.py:101
  17.9 2.4 fusion.58
  20.2 1.4 fusion.56
  21.6 3.9 %convolution_convert_fusion = bf16[768,2304]{1,0:T(8,128)(2,1)} fusion(bf16[512,768]{1,0:T(8,128)(2,1)S(1)} %get-tuple-element.19, bf16[512,768]{1,0:T(8,128)(2,1)S(1)} %get-tuple-element.28, bf16[512,768]{1,0:T(8,128)(2,1)S(1)} %get-tuple-element.15, s32[512]{0:T(512)S(1)} %multiply_add_fusion), kind=kOutput, calls=%fused_computation.19 | convolution fusion | flops 1821179904 | bytes 5900288 | tf_op jit(solution)/shard_map/dot_general | solution.py:71
  26.1 7.4 %all-to-all-start.1 = ((bf16[32,24,2304]{2,1,0:T(8,128)(2,1)}), bf16[32,24,2304]{2,1,0:T(8,128)(2,1)S(1)}, u32[]{:S(2)}, u32[]{:S(2)}) async-start(bf16[32,24,2304]{2,1,0:T(8,128)(2,1)} %bitcast.39), calls=%async_computation.1 | async-start | bytes 7077888 | tf_op jit(solution)/shard_map/all_to_all | solution.py:120
  33.5 5.5 %convolution_convert_fusion.1 = bf16[768,2304]{1,0:T(8,128)(2,1)} fusion(bf16[512,768]{1,0:T(8,128)(2,1)} %get-tuple-element.20, bf16[512,768]{1,0:T(8,128)(2,1)} %get-tuple-element.27, bf16[512,768]{1,0:T(8,128)(2,1)} %get-tuple-element.16, s32[512]{0:T(512)} %copy-done.7), kind=kOutput, calls=%fused_computation.20 | convolution fusion | flops 1821179904 | bytes 5900288 | tf_op jit(solution)/shard_map/dot_general | solution.py:71
  42.7 34.7 %all-to-all-done.1 = bf16[32,24,2304]{2,1,0:T(8,128)(2,1)S(1)} async-done(((bf16[32,24,2304]{2,1,0:T(8,128)(2,1)}), bf16[32,24,2304]{2,1,0:T(8,128)(2,1)S(1)}, u32[]{:S(2)}, u32[]{:S(2)}) %all-to-all-start.1) | async-done | bytes 3538976 | tf_op jit(solution)/shard_map/all_to_all | solution.py:120
  77.4 1.8 copy-done
  79.2 7.2 %all-to-all-start = ((bf16[32,24,2304]{2,1,0:T(8,128)(2,1)}), bf16[32,24,2304]{2,1,0:T(8,128)(2,1)}, u32[]{:S(2)}, u32[]{:S(2)}) async-start(bf16[32,24,2304]{2,1,0:T(8,128)(2,1)} %bitcast.38), calls=%async_computation | async-start | bytes 7077888 | tf_op jit(solution)/shard_map/all_to_all | solution.py:120
  86.8 3.6 %fusion.55 = (bf16[768,768]{1,0:T(8,128)(2,1)}, bf16[768,768]{1,0:T(8,128)(2,1)S(1)}, bf16[768,768]{1,0:T(8,128)(2,1)}) fusion(bf16[768,2304]{1,0:T(8,128)(2,1)} %bitcast.33), kind=kLoop, calls=%fused_computation.70 | loop fusion | bytes 7077888 | tf_op jit(solution)/shard_map/slice | solution.py:132
  91.1 1.6 copy.54
  92.7 2.4 copy.49
  95.1 6.4 %fusion = (f32[6,768]{1,0:T(8,128)S(1)}, f32[6,768,768]{1,2,0:T(8,128)}) fusion(pred[768,768]{0,1:T(8,128)(4,1)S(1)} %fusion.31, bf16[768,6,128]{0,2,1:T(8,128)(2,1)S(1)} %bitcast.34, bf16[768,6,128]{0,2,1:T(8,128)(2,1)S(1)} %bitcast.36), kind=kOutput, calls=%fused_computation.5 | convolution fusion | flops 916581888 | bytes 17123328 | tf_op jit(solution)/shard_map/qhd,khd->hqk/dot_general | solution.py:129
  101.5 8.0 %fusion.2 = f32[6,768]{1,0:T(8,128)S(1)} fusion(f32[6,768,768]{1,2,0:T(8,128)} %get-tuple-element.24, f32[6,768]{1,0:T(8,128)S(1)} %get-tuple-element.23, pred[768,768]{0,1:T(8,128)(4,1)S(1)} %fusion.31), kind=kLoop, calls=%fused_computation.7 | loop fusion | flops 14151168 | bytes 14782464 | tf_op jit(solution)/shard_map/reduce_sum | solution.py:138
  109.5 9.1 %fusion.29 = bf16[768,6,128]{0,2,1:T(8,128)(2,1)S(1)} fusion(bf16[768,6,128]{0,2,1:T(8,128)(2,1)S(1)} %bitcast.42, f32[6,768,768]{1,2,0:T(8,128)} %get-tuple-element.24, f32[6,768]{1,0:T(8,128)S(1)} %get-tuple-element.23, pred[768,768]{0,1:T(8,128)(4,1)S(1)} %fusion.31, f32[768,6]{0,1:T(8,128)S(1)} %bitcast.46), kind=kOutput, calls=%fused_computation.34 | convolution fusion | flops 921305088 | bytes 17141760 | tf_op jit(solution)/shard_map/hqk,khd->qhd/dot_general | solution.py:140
  118.6 1.1 copy.58
  119.8 2.2 reshape.228
  122.0 8.1 %all-to-all-done = bf16[32,24,2304]{2,1,0:T(8,128)(2,1)} async-done(((bf16[32,24,2304]{2,1,0:T(8,128)(2,1)}), bf16[32,24,2304]{2,1,0:T(8,128)(2,1)}, u32[]{:S(2)}, u32[]{:S(2)}) %all-to-all-start) | async-done | bytes 3538976 | tf_op jit(solution)/shard_map/all_to_all | solution.py:120
  130.1 3.6 %fusion.54 = (bf16[768,768]{1,0:T(8,128)(2,1)}, bf16[768,768]{1,0:T(8,128)(2,1)S(1)}, bf16[768,768]{1,0:T(8,128)(2,1)}) fusion(bf16[768,2304]{1,0:T(8,128)(2,1)} %bitcast.2), kind=kLoop, calls=%fused_computation.69 | loop fusion | bytes 7077888 | tf_op jit(solution)/shard_map/slice | solution.py:132
  134.4 1.6 copy.61
  136.0 2.4 copy.59
  138.3 6.4 %fusion.1 = (f32[6,768]{1,0:T(8,128)S(1)}, f32[6,768,768]{1,2,0:T(8,128)}) fusion(pred[768,768]{0,1:T(8,128)(4,1)S(1)} %fusion.31, bf16[768,6,128]{0,2,1:T(8,128)(2,1)S(1)} %bitcast.35, bf16[768,6,128]{0,2,1:T(8,128)(2,1)S(1)} %bitcast.37), kind=kOutput, calls=%fused_computation.6 | convolution fusion | flops 916581888 | bytes 17123328 | tf_op jit(solution)/shard_map/qhd,khd->hqk/dot_general | solution.py:129
  144.8 8.0 %fusion.4 = f32[6,768]{1,0:T(8,128)S(1)} fusion(f32[6,768,768]{1,2,0:T(8,128)} %get-tuple-element.26, f32[6,768]{1,0:T(8,128)S(1)} %get-tuple-element.25, pred[768,768]{0,1:T(8,128)(4,1)S(1)} %fusion.31), kind=kLoop, calls=%fused_computation.9 | loop fusion | flops 14151168 | bytes 14782464 | tf_op jit(solution)/shard_map/reduce_sum | solution.py:138
  152.8 9.1 %fusion.28 = bf16[768,6,128]{0,2,1:T(8,128)(2,1)S(1)} fusion(bf16[768,6,128]{0,2,1:T(8,128)(2,1)S(1)} %bitcast.41, f32[6,768,768]{1,2,0:T(8,128)} %get-tuple-element.26, f32[6,768]{1,0:T(8,128)S(1)} %get-tuple-element.25, pred[768,768]{0,1:T(8,128)(4,1)S(1)} %fusion.31, f32[768,6]{0,1:T(8,128)S(1)} %bitcast.45), kind=kOutput, calls=%fused_computation.32 | convolution fusion | flops 921305088 | bytes 17141760 | tf_op jit(solution)/shard_map/hqk,khd->qhd/dot_general | solution.py:140
  161.9 1.1 copy.65
  163.0 1.4 reshape.233
  164.5 25.4 %all_to_all.29 = bf16[32,24,768]{2,1,0:T(8,128)(2,1)} all-to-all(bf16[32,24,768]{2,1,0:T(8,128)(2,1)S(1)} %reshape.233), channel_id=1, replica_groups=mesh['head'=4,'seq'=32] {'seq'}, dimensions={0} | all-to-all | bytes 2359296 | tf_op jit(solution)/shard_map/all_to_all | solution.py:149
  189.8 4.1 %all-to-all-start.3 = ((bf16[32,24,768]{2,1,0:T(8,128)(2,1)}), bf16[32,24,768]{2,1,0:T(8,128)(2,1)S(1)}, u32[]{:S(2)}, u32[]{:S(2)}) async-start(bf16[32,24,768]{2,1,0:T(8,128)(2,1)} %reshape.228), calls=%async_computation.3 | async-start | bytes 2359296 | tf_op jit(solution)/shard_map/all_to_all | solution.py:123
  194.0 11.9 %fusion.6 = f32[512,6144]{1,0:T(8,128)} fusion(bf16[1536,6144]{1,0:T(8,128)(2,1)} %param.9, bf16[768,768]{1,0:T(8,128)(2,1)S(1)} %bitcast.43, s32[512]{0:T(512)S(1)} %copy-done.8), kind=kOutput, calls=%fused_computation.11 | convolution fusion | flops 5436604416 | bytes 23201792 | tf_op jit(solution)/shard_map/dot_general | solution.py:151
  205.9 6.7 %all-to-all-done.3 = bf16[32,24,768]{2,1,0:T(8,128)(2,1)S(1)} async-done(((bf16[32,24,768]{2,1,0:T(8,128)(2,1)}), bf16[32,24,768]{2,1,0:T(8,128)(2,1)S(1)}, u32[]{:S(2)}, u32[]{:S(2)}) %all-to-all-start.3) | async-done | bytes 1179680 | tf_op jit(solution)/shard_map/all_to_all | solution.py:123
  212.6 12.6 %add_convert_fusion = bf16[512,6144]{1,0:T(8,128)(2,1)} fusion(f32[512,6144]{1,0:T(8,128)} %fusion.6, bf16[1536,6144]{1,0:T(8,128)(2,1)} %param.9, bf16[768,768]{1,0:T(8,128)(2,1)S(1)} %bitcast.40, s32[512]{0:T(512)S(1)} %copy-done.8), kind=kOutput, calls=%fused_computation.4 | convolution fusion | flops 5442895872 | bytes 29493248 | tf_op jit(solution)/shard_map/dot_general | solution.py:125
  225.3 62.6 %reduce-scatter.2.cloned.1.call-done = bf16[512,1536]{1,0:T(8,128)(2,1)} async-done(((bf16[512,6144]{1,0:T(8,128)(2,1)}), bf16[512,1536]{1,0:T(8,128)(2,1)}) %reduce-scatter.2.cloned.1.call-update) | async-done | bytes 1572880 | tf_op jit(solution)/shard_map/reduce_scatter | solution.py:153
  (34 shorter events, 8.9 us)
Async XLA Ops:
  6.5 13.7 %copy-start.1 = (bf16[512,1536]{1,0:T(8,128)(2,1)S(1)}, bf16[512,1536]{1,0:T(8,128)(2,1)}, u32[]{:S(2)}) copy-start(bf16[512,1536]{1,0:T(8,128)(2,1)} %param.5) | copy-start | bytes 4718596
  6.5 13.7 %copy-start.2 = (bf16[512,1536]{1,0:T(8,128)(2,1)S(1)}, bf16[512,1536]{1,0:T(8,128)(2,1)}, u32[]{:S(2)}) copy-start(bf16[512,1536]{1,0:T(8,128)(2,1)} %param.6) | copy-start | bytes 4718596
  8.2 17.3 %all-to-all-start.2 = ((s32[32,1,8]{2,1,0:T(1,128)}), s32[32,1,8]{2,1,0:T(1,128)S(1)}, u32[]{:S(2)}, u32[]{:S(2)}) async-start(s32[32,1,8]{2,1,0:T(1,128)} %bitcast.6), calls=%async_computation.2 | async-start | bytes 32768 | tf_op jit(solution)/shard_map/all_to_all | solution.py:101
  17.8 3.7 %copy-start.7 = (s32[512]{0:T(512)}, s32[512]{0:T(512)S(1)}, u32[]{:S(2)}) copy-start(s32[512]{0:T(512)S(1)} %multiply_add_fusion) | copy-start | bytes 6148
  25.5 0.6 copy-start.6
  26.1 51.3 %all-to-all-start.1 = ((bf16[32,24,2304]{2,1,0:T(8,128)(2,1)}), bf16[32,24,2304]{2,1,0:T(8,128)(2,1)S(1)}, u32[]{:S(2)}, u32[]{:S(2)}) async-start(bf16[32,24,2304]{2,1,0:T(8,128)(2,1)} %bitcast.39), calls=%async_computation.1 | async-start | bytes 7077888 | tf_op jit(solution)/shard_map/all_to_all | solution.py:120
  77.4 1.8 copy-start
  79.2 50.9 %all-to-all-start = ((bf16[32,24,2304]{2,1,0:T(8,128)(2,1)}), bf16[32,24,2304]{2,1,0:T(8,128)(2,1)}, u32[]{:S(2)}, u32[]{:S(2)}) async-start(bf16[32,24,2304]{2,1,0:T(8,128)(2,1)} %bitcast.38), calls=%async_computation | async-start | bytes 7077888 | tf_op jit(solution)/shard_map/all_to_all | solution.py:120
  101.5 8.0 %copy-start.4 = (bf16[768,768]{0,1:T(8,128)(2,1)S(1)}, bf16[768,768]{0,1:T(8,128)(2,1)}, u32[]{:S(2)}) copy-start(bf16[768,768]{0,1:T(8,128)(2,1)} %copy.49) | copy-start | bytes 3538948
  144.8 8.0 %copy-start.3 = (bf16[768,768]{0,1:T(8,128)(2,1)S(1)}, bf16[768,768]{0,1:T(8,128)(2,1)}, u32[]{:S(2)}) copy-start(bf16[768,768]{0,1:T(8,128)(2,1)} %copy.59) | copy-start | bytes 3538948
  164.4 29.6 %copy-start.8 = (s32[512]{0:T(512)S(1)}, s32[512]{0:T(512)}, u32[]{:S(2)}) copy-start(s32[512]{0:T(512)} %copy-done.7) | copy-start | bytes 6148
  189.8 4.2 %copy-start.5 = (bf16[32,24,768]{2,1,0:T(8,128)(2,1)S(1)}, bf16[32,24,768]{2,1,0:T(8,128)(2,1)}, u32[]{:S(2)}) copy-start(bf16[32,24,768]{2,1,0:T(8,128)(2,1)} %all_to_all.29) | copy-start | bytes 3538948
  189.8 22.8 %all-to-all-start.3 = ((bf16[32,24,768]{2,1,0:T(8,128)(2,1)}), bf16[32,24,768]{2,1,0:T(8,128)(2,1)S(1)}, u32[]{:S(2)}, u32[]{:S(2)}) async-start(bf16[32,24,768]{2,1,0:T(8,128)(2,1)} %reshape.228), calls=%async_computation.3 | async-start | bytes 2359296 | tf_op jit(solution)/shard_map/all_to_all | solution.py:123
  194.0 93.9 %reduce-scatter.2.cloned.1.call-start = ((), (), s32[]{:S(2)}) async-start(), calls=%async_computation.6 | async-start | bytes 7864320 | tf_op jit(solution)/shard_map/reduce_scatter | solution.py:153
Sparse Core Ops, SparseCore 0:
  225.4 62.4 reduce-scatter.1

commit v2 on v1

--- a/solution.py
+++ b/solution.py
@@ -148,11 +148,16 @@
         prev_cols = cols
     returned = lax.all_to_all(back, "seq", 0, 0, tiled=True)
     own_rows = permute(to_token, returned.reshape(slots, part))
-    term = jnp.dot(own_rows, w_out[prev_cols], preferred_element_type=jnp.float32)
-    partial_value = term if partial_value is None else partial_value + term
-    summed = lax.psum_scatter(
-        partial_value.astype(jnp.bfloat16), "head", scatter_dimension=1, tiled=True
-    )
+    half = tokens // 2
+    outs = []
+    for lo in (0, half):
+        term = jnp.dot(own_rows[lo : lo + half], w_out[prev_cols], preferred_element_type=jnp.float32)
+        if partial_value is not None:
+            term = partial_value[lo : lo + half] + term
+        outs.append(
+            lax.psum_scatter(term.astype(jnp.bfloat16), "head", scatter_dimension=1, tiled=True)
+        )
+    summed = jnp.concatenate(outs, axis=0)
     return summed
 
 

time: 296 us -> 328 us (1.11); the launches traced: 295 us -> 322 us
  waiting for transfers between devices: 112 us -> 127 us
  matrix products: 64.8 us -> 74 us
    dot_general x0 -> x2, matrix products: none -> 19.5 us  [body(): jnp.dot(own_rows[lo:lo + half], w_out[prev_cols], preferred_element_type=...]
    dot_general x2 -> x1, matrix products: 24.5 us -> 11.9 us  [body(): jnp.dot(own_rows, w_out[prev_cols], preferred_element_type=jnp.float32)]
    all_to_all x1, waiting for transfers between devices: 6.69 us -> 16.5 us  [body(): returned = lax.all_to_all(back, 'seq', 0, 0, tiled=True)]
    reduce_scatter x1 -> x2, waiting for transfers between devices: 62.6 us -> 67.6 us  [body(): lax.psum_scatter(term.astype(jnp.bfloat16), 'head', scatter_dimension=1,...]
    dot_general x2 -> x3, matrix products: 9.39 us -> 11.5 us  [permute(): jnp.dot(selector, block, preferred_element_type=jnp.float32)]
  transfers between devices with their start and end apart: 5 -> 6, of which waited for: 4 -> 5; matrix products, arithmetic and copies ran while one was open for 22% -> 20% of each run, Pallas kernels for 0% -> 0%
where the time goes in v2:
time: 328 us; the launch traced here: 322 us
  waiting for transfers between devices  127 us (39%)
  matrix products  74 us (23%)
  local copies, waits for them, and re-layouts  31.3 us (10%)
  starting transfers between devices  27.8 us (8%)
  blocking collectives  25.4 us (8%)
  other arithmetic  22.8 us (7%)
  between operations  13.8 us (4%)
    reduce_scatter x2, waiting for transfers between devices, body(): lax.psum_scatter(term.astype(jnp.bfloat16), 'head', scatter_dimension=1,...  67.6 us
    all_to_all x2, waiting for transfers between devices, body(): lax.all_to_all(outgoing, 'seq', 0, 0, tiled=True).reshape(slots, 3 * part)  42.7 us
    all_to_all x1, blocking collectives, body(): returned = lax.all_to_all(back, 'seq', 0, 0, tiled=True)  25.4 us
    dot_general x2, matrix products, body(): jnp.dot(own_rows[lo:lo + half], w_out[prev_cols], preferred_element_type=...  19.5 us
    dot_general x2, matrix products, body(): jnp.einsum('hqk,khd->qhd', weights, incoming[:, 2 * part:].reshape(head_s...  18.1 us
    all_to_all x1, waiting for transfers between devices, body(): returned = lax.all_to_all(back, 'seq', 0, 0, tiled=True)  16.5 us
    reduce_sum x2, other arithmetic, body(): totals = jnp.sum(exp_scores, axis=-1)  16.1 us
    all_to_all x2, starting transfers between devices, body(): lax.all_to_all(outgoing, 'seq', 0, 0, tiled=True).reshape(slots, 3 * part)  15.2 us
  transfers between devices with their start and end apart: 6, of which 5 were waited for; matrix products, arithmetic and copies ran while one was open for 20% of the time, Pallas kernels for 0%

profile of v2, /device:TPU:1, one launch (start us, length us, event | category | flops | bytes accessed | tf_op | source)
XLA Modules:
  0.0 321.9 jit_solution(10284963558994765386)
XLA Ops:
  8.2 8.6 %all-to-all-start.2 = ((s32[32,1,8]{2,1,0:T(1,128)}), s32[32,1,8]{2,1,0:T(1,128)S(1)}, u32[]{:S(2)}, u32[]{:S(2)}) async-start(s32[32,1,8]{2,1,0:T(1,128)} %bitcast.6), calls=%async_computation.2 | async-start | bytes 32768 | tf_op jit(solution)/shard_map/all_to_all | solution.py:101
  17.9 2.4 fusion.71
  21.6 3.9 %convolution_convert_fusion = bf16[768,2304]{1,0:T(8,128)(2,1)} fusion(bf16[512,768]{1,0:T(8,128)(2,1)S(1)} %get-tuple-element.19, bf16[512,768]{1,0:T(8,128)(2,1)S(1)} %get-tuple-element.28, bf16[512,768]{1,0:T(8,128)(2,1)S(1)} %get-tuple-element.15, s32[512]{0:T(512)S(1)} %multiply_add_fusion), kind=kOutput, calls=%fused_computation.24 | convolution fusion | flops 1821179904 | bytes 5900288 | tf_op jit(solution)/shard_map/dot_general | solution.py:71
  26.1 7.4 %all-to-all-start.1 = ((bf16[32,24,2304]{2,1,0:T(8,128)(2,1)}), bf16[32,24,2304]{2,1,0:T(8,128)(2,1)S(1)}, u32[]{:S(2)}, u32[]{:S(2)}) async-start(bf16[32,24,2304]{2,1,0:T(8,128)(2,1)} %bitcast.39), calls=%async_computation.1 | async-start | bytes 7077888 | tf_op jit(solution)/shard_map/all_to_all | solution.py:120
  33.5 5.5 %convolution_convert_fusion.1 = bf16[768,2304]{1,0:T(8,128)(2,1)} fusion(bf16[512,768]{1,0:T(8,128)(2,1)} %get-tuple-element.20, bf16[512,768]{1,0:T(8,128)(2,1)} %get-tuple-element.27, bf16[512,768]{1,0:T(8,128)(2,1)} %get-tuple-element.16, s32[512]{0:T(512)} %copy-done.6), kind=kOutput, calls=%fused_computation.25 | convolution fusion | flops 1821179904 | bytes 5900288 | tf_op jit(solution)/shard_map/dot_general | solution.py:71
  42.7 34.7 %all-to-all-done.1 = bf16[32,24,2304]{2,1,0:T(8,128)(2,1)S(1)} async-done(((bf16[32,24,2304]{2,1,0:T(8,128)(2,1)}), bf16[32,24,2304]{2,1,0:T(8,128)(2,1)S(1)}, u32[]{:S(2)}, u32[]{:S(2)}) %all-to-all-start.1) | async-done | bytes 3538976 | tf_op jit(solution)/shard_map/all_to_all | solution.py:120
  77.4 1.8 copy-done
  79.2 7.8 %all-to-all-start = ((bf16[32,24,2304]{2,1,0:T(8,128)(2,1)}), bf16[32,24,2304]{2,1,0:T(8,128)(2,1)}, u32[]{:S(2)}, u32[]{:S(2)}) async-start(bf16[32,24,2304]{2,1,0:T(8,128)(2,1)} %bitcast.38), calls=%async_computation | async-start | bytes 7077888 | tf_op jit(solution)/shard_map/all_to_all | solution.py:120
  87.5 3.6 %fusion.68 = (bf16[768,768]{1,0:T(8,128)(2,1)}, bf16[768,768]{1,0:T(8,128)(2,1)S(1)}, bf16[768,768]{1,0:T(8,128)(2,1)}) fusion(bf16[768,2304]{1,0:T(8,128)(2,1)} %bitcast.33), kind=kLoop, calls=%fused_computation.78 | loop fusion | bytes 7077888 | tf_op jit(solution)/shard_map/slice | solution.py:132
  91.7 1.6 copy.54
  93.3 2.4 copy.49
  95.7 6.4 %fusion = (f32[6,768]{1,0:T(8,128)S(1)}, f32[6,768,768]{1,2,0:T(8,128)}) fusion(pred[768,768]{0,1:T(8,128)(4,1)S(1)} %fusion.43, bf16[768,6,128]{0,2,1:T(8,128)(2,1)S(1)} %bitcast.34, bf16[768,6,128]{0,2,1:T(8,128)(2,1)S(1)} %bitcast.36), kind=kOutput, calls=%fused_computation.4 | convolution fusion | flops 916581888 | bytes 17123328 | tf_op jit(solution)/shard_map/qhd,khd->hqk/dot_general | solution.py:129
  102.1 8.0 %fusion.2 = f32[6,768]{1,0:T(8,128)S(1)} fusion(f32[6,768,768]{1,2,0:T(8,128)} %get-tuple-element.24, f32[6,768]{1,0:T(8,128)S(1)} %get-tuple-element.23, pred[768,768]{0,1:T(8,128)(4,1)S(1)} %fusion.43), kind=kLoop, calls=%fused_computation.6 | loop fusion | flops 14151168 | bytes 14782464 | tf_op jit(solution)/shard_map/reduce_sum | solution.py:138
  110.2 9.1 %fusion.41 = bf16[768,6,128]{0,2,1:T(8,128)(2,1)S(1)} fusion(bf16[768,6,128]{0,2,1:T(8,128)(2,1)S(1)} %bitcast.42, f32[6,768,768]{1,2,0:T(8,128)} %get-tuple-element.24, f32[6,768]{1,0:T(8,128)S(1)} %get-tuple-element.23, pred[768,768]{0,1:T(8,128)(4,1)S(1)} %fusion.43, f32[768,6]{0,1:T(8,128)S(1)} %bitcast.46), kind=kOutput, calls=%fused_computation.39 | convolution fusion | flops 921305088 | bytes 17141760 | tf_op jit(solution)/shard_map/hqk,khd->qhd/dot_general | solution.py:140
  120.4 2.2 reshape.228
  122.6 8.0 %all-to-all-done = bf16[32,24,2304]{2,1,0:T(8,128)(2,1)} async-done(((bf16[32,24,2304]{2,1,0:T(8,128)(2,1)}), bf16[32,24,2304]{2,1,0:T(8,128)(2,1)}, u32[]{:S(2)}, u32[]{:S(2)}) %all-to-all-start) | async-done | bytes 3538976 | tf_op jit(solution)/shard_map/all_to_all | solution.py:120
  130.5 3.6 %fusion.67 = (bf16[768,768]{1,0:T(8,128)(2,1)}, bf16[768,768]{1,0:T(8,128)(2,1)S(1)}, bf16[768,768]{1,0:T(8,128)(2,1)}) fusion(bf16[768,2304]{1,0:T(8,128)(2,1)} %bitcast.2), kind=kLoop, calls=%fused_computation.77 | loop fusion | bytes 7077888 | tf_op jit(solution)/shard_map/slice | solution.py:132
  134.8 1.6 copy.61
  136.4 2.4 copy.59
  138.8 6.6 %fusion.1 = (f32[6,768]{1,0:T(8,128)S(1)}, f32[6,768,768]{1,2,0:T(8,128)}) fusion(pred[768,768]{0,1:T(8,128)(4,1)S(1)} %fusion.43, bf16[768,6,128]{0,2,1:T(8,128)(2,1)S(1)} %bitcast.35, bf16[768,6,128]{0,2,1:T(8,128)(2,1)S(1)} %bitcast.37), kind=kOutput, calls=%fused_computation.5 | convolution fusion | flops 916581888 | bytes 17123328 | tf_op jit(solution)/shard_map/qhd,khd->hqk/dot_general | solution.py:129
  145.4 8.0 %fusion.4 = f32[6,768]{1,0:T(8,128)S(1)} fusion(f32[6,768,768]{1,2,0:T(8,128)} %get-tuple-element.26, f32[6,768]{1,0:T(8,128)S(1)} %get-tuple-element.25, pred[768,768]{0,1:T(8,128)(4,1)S(1)} %fusion.43), kind=kLoop, calls=%fused_computation.8 | loop fusion | flops 14151168 | bytes 14782464 | tf_op jit(solution)/shard_map/reduce_sum | solution.py:138
  153.4 9.1 %fusion.40 = bf16[768,6,128]{0,2,1:T(8,128)(2,1)S(1)} fusion(bf16[768,6,128]{0,2,1:T(8,128)(2,1)S(1)} %bitcast.41, f32[6,768,768]{1,2,0:T(8,128)} %get-tuple-element.26, f32[6,768]{1,0:T(8,128)S(1)} %get-tuple-element.25, pred[768,768]{0,1:T(8,128)(4,1)S(1)} %fusion.43, f32[768,6]{0,1:T(8,128)S(1)} %bitcast.45), kind=kOutput, calls=%fused_computation.37 | convolution fusion | flops 921305088 | bytes 17141760 | tf_op jit(solution)/shard_map/hqk,khd->qhd/dot_general | solution.py:140
  165.1 25.4 %all_to_all.29 = bf16[32,24,768]{2,1,0:T(8,128)(2,1)} all-to-all(bf16[32,24,768]{2,1,0:T(8,128)(2,1)S(1)} %reshape.233), channel_id=1, replica_groups=mesh['head'=4,'seq'=32] {'seq'}, dimensions={0} | all-to-all | bytes 2359296 | tf_op jit(solution)/shard_map/all_to_all | solution.py:149
  190.5 4.0 %all-to-all-start.3 = ((bf16[32,24,768]{2,1,0:T(8,128)(2,1)}), bf16[32,24,768]{2,1,0:T(8,128)(2,1)S(1)}, u32[]{:S(2)}, u32[]{:S(2)}) async-start(bf16[32,24,768]{2,1,0:T(8,128)(2,1)} %reshape.228), calls=%async_computation.3 | async-start | bytes 2359296 | tf_op jit(solution)/shard_map/all_to_all | solution.py:123
  194.5 2.1 fusion.51
  196.7 16.5 %all-to-all-done.3 = bf16[32,24,768]{2,1,0:T(8,128)(2,1)S(1)} async-done(((bf16[32,24,768]{2,1,0:T(8,128)(2,1)}), bf16[32,24,768]{2,1,0:T(8,128)(2,1)S(1)}, u32[]{:S(2)}, u32[]{:S(2)}) %all-to-all-start.3) | async-done | bytes 1179680 | tf_op jit(solution)/shard_map/all_to_all | solution.py:123
  213.1 11.9 %fusion.6 = f32[512,6144]{1,0:T(8,128)} fusion(bf16[1536,6144]{1,0:T(8,128)(2,1)} %param.9, bf16[768,768]{1,0:T(8,128)(2,1)S(1)} %bitcast.40, s32[512]{0:T(512)S(1)} %copy-done.7), kind=kOutput, calls=%fused_computation.10 | convolution fusion | flops 5436604416 | bytes 23201792 | tf_op jit(solution)/shard_map/dot_general | solution.py:125
  225.0 9.8 %fusion.21 = bf16[256,6144]{1,0:T(8,128)(2,1)} fusion(bf16[1536,6144]{1,0:T(8,128)(2,1)} %param.9, f32[512,6144]{1,0:T(8,128)} %fusion.6, bf16[512,768]{1,0:T(8,128)(2,1)S(1)} %fusion.51), kind=kOutput, calls=%fused_computation.19 | convolution fusion | flops 2419064832 | bytes 19267584 | tf_op jit(solution)/shard_map/dot_general | solution.py:154
  234.8 9.8 %fusion.18 = bf16[256,6144]{1,0:T(8,128)(2,1)} fusion(bf16[1536,6144]{1,0:T(8,128)(2,1)} %param.9, f32[512,6144]{1,0:T(8,128)} %fusion.6, bf16[512,768]{1,0:T(8,128)(2,1)S(1)} %fusion.51), kind=kOutput, calls=%fused_computation.18 | convolution fusion | flops 2419064832 | bytes 19267584 | tf_op jit(solution)/shard_map/dot_general | solution.py:154
  244.6 27.1 %reduce-scatter.3.cloned.1.call-done = bf16[256,1536]{1,0:T(8,128)(2,1)} async-done(((bf16[256,6144]{1,0:T(8,128)(2,1)}), bf16[256,1536]{1,0:T(8,128)(2,1)}) %reduce-scatter.3.cloned.1.call-update) | async-done | bytes 786448 | tf_op jit(solution)/shard_map/reduce_scatter | solution.py:158
  271.7 40.5 %reduce-scatter.5.cloned.1.call-done = bf16[256,1536]{1,0:T(8,128)(2,1)} async-done(((bf16[256,6144]{1,0:T(8,128)(2,1)}), bf16[256,1536]{1,0:T(8,128)(2,1)}) %reduce-scatter.5.cloned.1.call-update) | async-done | bytes 786448 | tf_op jit(solution)/shard_map/reduce_scatter | solution.py:158
  312.2 2.6 pad_maximum_fusion
  (38 shorter events, 14.0 us)
Async XLA Ops:
  6.5 13.7 %copy-start.1 = (bf16[512,1536]{1,0:T(8,128)(2,1)S(1)}, bf16[512,1536]{1,0:T(8,128)(2,1)}, u32[]{:S(2)}) copy-start(bf16[512,1536]{1,0:T(8,128)(2,1)} %param.5) | copy-start | bytes 4718596
  6.5 13.7 %copy-start.2 = (bf16[512,1536]{1,0:T(8,128)(2,1)S(1)}, bf16[512,1536]{1,0:T(8,128)(2,1)}, u32[]{:S(2)}) copy-start(bf16[512,1536]{1,0:T(8,128)(2,1)} %param.6) | copy-start | bytes 4718596
  8.2 17.3 %all-to-all-start.2 = ((s32[32,1,8]{2,1,0:T(1,128)}), s32[32,1,8]{2,1,0:T(1,128)S(1)}, u32[]{:S(2)}, u32[]{:S(2)}) async-start(s32[32,1,8]{2,1,0:T(1,128)} %bitcast.6), calls=%async_computation.2 | async-start | bytes 32768 | tf_op jit(solution)/shard_map/all_to_all | solution.py:101
  17.8 3.7 %copy-start.6 = (s32[512]{0:T(512)}, s32[512]{0:T(512)S(1)}, u32[]{:S(2)}) copy-start(s32[512]{0:T(512)S(1)} %multiply_add_fusion) | copy-start | bytes 6148
  25.5 0.6 copy-start.5
  26.1 51.3 %all-to-all-start.1 = ((bf16[32,24,2304]{2,1,0:T(8,128)(2,1)}), bf16[32,24,2304]{2,1,0:T(8,128)(2,1)S(1)}, u32[]{:S(2)}, u32[]{:S(2)}) async-start(bf16[32,24,2304]{2,1,0:T(8,128)(2,1)} %bitcast.39), calls=%async_computation.1 | async-start | bytes 7077888 | tf_op jit(solution)/shard_map/all_to_all | solution.py:120
  77.4 1.8 copy-start
  79.2 51.3 %all-to-all-start = ((bf16[32,24,2304]{2,1,0:T(8,128)(2,1)}), bf16[32,24,2304]{2,1,0:T(8,128)(2,1)}, u32[]{:S(2)}, u32[]{:S(2)}) async-start(bf16[32,24,2304]{2,1,0:T(8,128)(2,1)} %bitcast.38), calls=%async_computation | async-start | bytes 7077888 | tf_op jit(solution)/shard_map/all_to_all | solution.py:120
  102.1 8.0 %copy-start.4 = (bf16[768,768]{0,1:T(8,128)(2,1)S(1)}, bf16[768,768]{0,1:T(8,128)(2,1)}, u32[]{:S(2)}) copy-start(bf16[768,768]{0,1:T(8,128)(2,1)} %copy.49) | copy-start | bytes 3538948
  145.4 8.0 %copy-start.3 = (bf16[768,768]{0,1:T(8,128)(2,1)S(1)}, bf16[768,768]{0,1:T(8,128)(2,1)}, u32[]{:S(2)}) copy-start(bf16[768,768]{0,1:T(8,128)(2,1)} %copy.59) | copy-start | bytes 3538948
  163.7 30.9 %copy-start.7 = (s32[512]{0:T(512)S(1)}, s32[512]{0:T(512)}, u32[]{:S(2)}) copy-start(s32[512]{0:T(512)} %copy-done.6) | copy-start | bytes 6148
  190.5 22.7 %all-to-all-start.3 = ((bf16[32,24,768]{2,1,0:T(8,128)(2,1)}), bf16[32,24,768]{2,1,0:T(8,128)(2,1)S(1)}, u32[]{:S(2)}, u32[]{:S(2)}) async-start(bf16[32,24,768]{2,1,0:T(8,128)(2,1)} %reshape.228), calls=%async_computation.3 | async-start | bytes 2359296 | tf_op jit(solution)/shard_map/all_to_all | solution.py:123
  194.5 77.2 %reduce-scatter.3.cloned.1.call-start = ((), (), s32[]{:S(2)}) async-start(), calls=%async_computation.7 | async-start | bytes 3932160 | tf_op jit(solution)/shard_map/reduce_scatter | solution.py:158
  234.8 77.5 %reduce-scatter.5.cloned.1.call-start = ((), (), s32[]{:S(2)}) async-start(), calls=%async_computation.8 | async-start | bytes 3932160 | tf_op jit(solution)/shard_map/reduce_scatter | solution.py:158
Sparse Core Ops, SparseCore 0:
  234.9 36.7 reduce-scatter.2
  274.1 38.0 reduce-scatter.4

commit v3 on v1

--- a/solution.py
+++ b/solution.py
@@ -120,10 +120,8 @@
         incoming = lax.all_to_all(outgoing, "seq", 0, 0, tiled=True).reshape(slots, 3 * part)
         if k > 0:
             incoming, back = lax.optimization_barrier((incoming, back))
-            returned = lax.all_to_all(back, "seq", 0, 0, tiled=True)
-            own_rows = permute(to_token, returned.reshape(slots, part))
-            term = jnp.dot(own_rows, w_out[prev_cols], preferred_element_type=jnp.float32)
-            partial_value = term if partial_value is None else partial_value + term
+            returned_prev = lax.all_to_all(back, "seq", 0, 0, tiled=True)
+            done_cols = prev_cols
         heads_part = part // HD
         head_shape = (slots, heads_part, HD)
         scores = jnp.einsum(
@@ -145,6 +143,11 @@
         )
         attended = attended / totals.T[:, :, None]
         back = attended.astype(jnp.bfloat16).reshape(seq_count, rows, part)
+        if k > 0:
+            back, returned_prev = lax.optimization_barrier((back, returned_prev))
+            own_rows = permute(to_token, returned_prev.reshape(slots, part))
+            term = jnp.dot(own_rows, w_out[done_cols], preferred_element_type=jnp.float32)
+            partial_value = term if partial_value is None else partial_value + term
         prev_cols = cols
     returned = lax.all_to_all(back, "seq", 0, 0, tiled=True)
     own_rows = permute(to_token, returned.reshape(slots, part))

time: 296 us -> 293 us (0.990)
  waiting for transfers between devices: 112 us -> 106 us
  starting transfers between devices: 27.3 us -> 30.7 us
    dot_general x2 -> x1, matrix products: 24.5 us -> 11.7 us  [body(): jnp.dot(own_rows, w_out[prev_cols], preferred_element_type=jnp.float32)]
    dot_general x0 -> x1, matrix products: none -> 12.8 us  [body(): jnp.dot(own_rows, w_out[done_cols], preferred_element_type=jnp.float32)]
    all_to_all x1, waiting for transfers between devices: 6.69 us -> 0.01 us  [body(): returned_prev = lax.all_to_all(back, 'seq', 0, 0, tiled=True)]
    all_to_all x1, starting transfers between devices: 4.13 us -> 7.54 us  [body(): returned_prev = lax.all_to_all(back, 'seq', 0, 0, tiled=True)]
  transfers between devices with their start and end apart: 5 -> 5, of which waited for: 4 -> 3; matrix products, arithmetic and copies ran while one was open for 22% -> 27% of each run, Pallas kernels for 0% -> 0%
where the time goes in v3:
time: 293 us; the launch traced here: 292 us
  waiting for transfers between devices  106 us (36%)
  matrix products  64.8 us (22%)
  local copies, waits for them, and re-layouts  31.2 us (11%)
  starting transfers between devices  30.7 us (10%)
  blocking collectives  26.1 us (9%)
  other arithmetic  20.2 us (7%)
  between operations  13.6 us (5%)
    reduce_scatter x1, waiting for transfers between devices, body(): lax.psum_scatter(partial_value.astype(jnp.bfloat16), 'head', scatter_dime...  62.7 us
    all_to_all x2, waiting for transfers between devices, body(): lax.all_to_all(outgoing, 'seq', 0, 0, tiled=True).reshape(slots, 3 * part)  42.9 us
    all_to_all x1, blocking collectives, body(): returned = lax.all_to_all(back, 'seq', 0, 0, tiled=True)  26.1 us
    dot_general x2, matrix products, body(): jnp.einsum('hqk,khd->qhd', weights, incoming[:, 2 * part:].reshape(head_s...  18.1 us
    reduce_sum x2, other arithmetic, body(): totals = jnp.sum(exp_scores, axis=-1)  16.1 us
    all_to_all x2, starting transfers between devices, body(): lax.all_to_all(outgoing, 'seq', 0, 0, tiled=True).reshape(slots, 3 * part)  14.6 us
    dot_general x2, matrix products, body(): jnp.einsum('qhd,khd->hqk', incoming[:, :part].reshape(head_shape), incomi...  12.8 us
    dot_general x1, matrix products, body(): jnp.dot(own_rows, w_out[done_cols], preferred_element_type=jnp.float32)  12.8 us
  transfers between devices with their start and end apart: 5, of which 3 were waited for; matrix products, arithmetic and copies ran while one was open for 27% of the time, Pallas kernels for 0%

profile of v3, /device:TPU:1, one launch (start us, length us, event | category | flops | bytes accessed | tf_op | source)
XLA Modules:
  0.0 292.3 jit_solution(409467079452736727)
XLA Ops:
  6.5 1.0 convert_reduce_fusion.1
  8.2 8.6 %all-to-all-start.2 = ((s32[32,1,8]{2,1,0:T(1,128)}), s32[32,1,8]{2,1,0:T(1,128)S(1)}, u32[]{:S(2)}, u32[]{:S(2)}) async-start(s32[32,1,8]{2,1,0:T(1,128)} %bitcast.6), calls=%async_computation.2 | async-start | bytes 32768 | tf_op jit(solution)/shard_map/all_to_all | solution.py:101
  17.9 2.4 fusion.58
  20.2 1.4 fusion.56
  21.6 3.9 %convolution_convert_fusion = bf16[768,2304]{1,0:T(8,128)(2,1)} fusion(bf16[512,768]{1,0:T(8,128)(2,1)S(1)} %get-tuple-element.23, bf16[512,768]{1,0:T(8,128)(2,1)S(1)} %get-tuple-element.32, bf16[512,768]{1,0:T(8,128)(2,1)S(1)} %get-tuple-element.19, s32[512]{0:T(512)S(1)} %multiply_add_fusion), kind=kOutput, calls=%fused_computation.19 | convolution fusion | flops 1821179904 | bytes 5900288 | tf_op jit(solution)/shard_map/dot_general | solution.py:71
  26.1 7.4 %all-to-all-start.1 = ((bf16[32,24,2304]{2,1,0:T(8,128)(2,1)}), bf16[32,24,2304]{2,1,0:T(8,128)(2,1)S(1)}, u32[]{:S(2)}, u32[]{:S(2)}) async-start(bf16[32,24,2304]{2,1,0:T(8,128)(2,1)} %bitcast.39), calls=%async_computation.1 | async-start | bytes 7077888 | tf_op jit(solution)/shard_map/all_to_all | solution.py:120
  33.5 5.5 %convolution_convert_fusion.1 = bf16[768,2304]{1,0:T(8,128)(2,1)} fusion(bf16[512,768]{1,0:T(8,128)(2,1)} %get-tuple-element.24, bf16[512,768]{1,0:T(8,128)(2,1)} %get-tuple-element.31, bf16[512,768]{1,0:T(8,128)(2,1)} %get-tuple-element.20, s32[512]{0:T(512)} %copy-done.6), kind=kOutput, calls=%fused_computation.20 | convolution fusion | flops 1821179904 | bytes 5900288 | tf_op jit(solution)/shard_map/dot_general | solution.py:71
  42.7 34.7 %all-to-all-done.1 = bf16[32,24,2304]{2,1,0:T(8,128)(2,1)S(1)} async-done(((bf16[32,24,2304]{2,1,0:T(8,128)(2,1)}), bf16[32,24,2304]{2,1,0:T(8,128)(2,1)S(1)}, u32[]{:S(2)}, u32[]{:S(2)}) %all-to-all-start.1) | async-done | bytes 3538976 | tf_op jit(solution)/shard_map/all_to_all | solution.py:120
  77.4 1.8 copy-done
  79.2 7.2 %all-to-all-start = ((bf16[32,24,2304]{2,1,0:T(8,128)(2,1)}), bf16[32,24,2304]{2,1,0:T(8,128)(2,1)}, u32[]{:S(2)}, u32[]{:S(2)}) async-start(bf16[32,24,2304]{2,1,0:T(8,128)(2,1)} %bitcast.38), calls=%async_computation | async-start | bytes 7077888 | tf_op jit(solution)/shard_map/all_to_all | solution.py:120
  86.9 3.6 %fusion.55 = (bf16[768,768]{1,0:T(8,128)(2,1)}, bf16[768,768]{1,0:T(8,128)(2,1)S(1)}, bf16[768,768]{1,0:T(8,128)(2,1)}) fusion(bf16[768,2304]{1,0:T(8,128)(2,1)} %bitcast.33), kind=kLoop, calls=%fused_computation.70 | loop fusion | bytes 7077888 | tf_op jit(solution)/shard_map/slice | solution.py:130
  91.1 1.6 copy.54
  92.7 2.4 copy.49
  95.1 6.4 %fusion = (f32[6,768]{1,0:T(8,128)S(1)}, f32[6,768,768]{1,2,0:T(8,128)}) fusion(pred[768,768]{0,1:T(8,128)(4,1)S(1)} %fusion.31, bf16[768,6,128]{0,2,1:T(8,128)(2,1)S(1)} %bitcast.36, bf16[768,6,128]{0,2,1:T(8,128)(2,1)S(1)} %bitcast.37), kind=kOutput, calls=%fused_computation.5 | convolution fusion | flops 916581888 | bytes 17123328 | tf_op jit(solution)/shard_map/qhd,khd->hqk/dot_general | solution.py:127
  101.5 8.0 %fusion.2 = f32[6,768]{1,0:T(8,128)S(1)} fusion(f32[6,768,768]{1,2,0:T(8,128)} %get-tuple-element.28, f32[6,768]{1,0:T(8,128)S(1)} %get-tuple-element.27, pred[768,768]{0,1:T(8,128)(4,1)S(1)} %fusion.31), kind=kLoop, calls=%fused_computation.7 | loop fusion | flops 14151168 | bytes 14782464 | tf_op jit(solution)/shard_map/reduce_sum | solution.py:136
  109.5 9.1 %fusion.29 = bf16[768,6,128]{0,2,1:T(8,128)(2,1)S(1)} fusion(bf16[768,6,128]{0,2,1:T(8,128)(2,1)S(1)} %bitcast.41, f32[6,768,768]{1,2,0:T(8,128)} %get-tuple-element.28, f32[6,768]{1,0:T(8,128)S(1)} %get-tuple-element.27, pred[768,768]{0,1:T(8,128)(4,1)S(1)} %fusion.31, f32[768,6]{0,1:T(8,128)S(1)} %bitcast.45), kind=kOutput, calls=%fused_computation.34 | convolution fusion | flops 921305088 | bytes 17141760 | tf_op jit(solution)/shard_map/hqk,khd->qhd/dot_general | solution.py:138
  118.6 1.1 copy.58
  119.8 2.2 reshape.228
  122.0 8.2 %all-to-all-done = bf16[32,24,2304]{2,1,0:T(8,128)(2,1)} async-done(((bf16[32,24,2304]{2,1,0:T(8,128)(2,1)}), bf16[32,24,2304]{2,1,0:T(8,128)(2,1)}, u32[]{:S(2)}, u32[]{:S(2)}) %all-to-all-start) | async-done | bytes 3538976 | tf_op jit(solution)/shard_map/all_to_all | solution.py:120
  130.1 3.6 %fusion.54 = (bf16[768,768]{1,0:T(8,128)(2,1)}, bf16[768,768]{1,0:T(8,128)(2,1)S(1)}, bf16[768,768]{1,0:T(8,128)(2,1)}) fusion(bf16[768,2304]{1,0:T(8,128)(2,1)} %bitcast.2), kind=kLoop, calls=%fused_computation.69 | loop fusion | bytes 7077888 | tf_op jit(solution)/shard_map/slice | solution.py:130
  134.4 1.6 copy.61
  136.0 2.4 copy.59
  138.4 7.5 %all-to-all-start.3 = ((bf16[32,24,768]{2,1,0:T(8,128)(2,1)}), bf16[32,24,768]{2,1,0:T(8,128)(2,1)}, u32[]{:S(2)}, u32[]{:S(2)}) async-start(bf16[32,24,768]{2,1,0:T(8,128)(2,1)} %reshape.228), calls=%async_computation.3 | async-start | bytes 2359296 | tf_op jit(solution)/shard_map/all_to_all | solution.py:123
  146.0 6.4 %fusion.1 = (f32[6,768]{1,0:T(8,128)S(1)}, f32[6,768,768]{1,2,0:T(8,128)}) fusion(pred[768,768]{0,1:T(8,128)(4,1)S(1)} %fusion.31, bf16[768,6,128]{0,2,1:T(8,128)(2,1)S(1)} %bitcast.34, bf16[768,6,128]{0,2,1:T(8,128)(2,1)S(1)} %bitcast.35), kind=kOutput, calls=%fused_computation.6 | convolution fusion | flops 916581888 | bytes 17123328 | tf_op jit(solution)/shard_map/qhd,khd->hqk/dot_general | solution.py:127
  152.4 8.0 %fusion.4 = f32[6,768]{1,0:T(8,128)S(1)} fusion(f32[6,768,768]{1,2,0:T(8,128)} %get-tuple-element.30, f32[6,768]{1,0:T(8,128)S(1)} %get-tuple-element.29, pred[768,768]{0,1:T(8,128)(4,1)S(1)} %fusion.31), kind=kLoop, calls=%fused_computation.9 | loop fusion | flops 14151168 | bytes 14782464 | tf_op jit(solution)/shard_map/reduce_sum | solution.py:136
  160.4 9.1 %fusion.28 = bf16[768,6,128]{0,2,1:T(8,128)(2,1)S(1)} fusion(bf16[768,6,128]{0,2,1:T(8,128)(2,1)S(1)} %bitcast.40, f32[6,768,768]{1,2,0:T(8,128)} %get-tuple-element.30, f32[6,768]{1,0:T(8,128)S(1)} %get-tuple-element.29, pred[768,768]{0,1:T(8,128)(4,1)S(1)} %fusion.31, f32[768,6]{0,1:T(8,128)S(1)} %bitcast.44), kind=kOutput, calls=%fused_computation.32 | convolution fusion | flops 921305088 | bytes 17141760 | tf_op jit(solution)/shard_map/hqk,khd->qhd/dot_general | solution.py:138
  169.5 1.1 copy.65
  170.7 1.4 reshape.232
  172.1 26.1 %all_to_all.29 = bf16[32,24,768]{2,1,0:T(8,128)(2,1)S(1)} all-to-all(bf16[32,24,768]{2,1,0:T(8,128)(2,1)S(1)} %reshape.232), channel_id=1, replica_groups=mesh['head'=4,'seq'=32] {'seq'}, dimensions={0} | all-to-all | bytes 2359296 | tf_op jit(solution)/shard_map/all_to_all | solution.py:152
  198.2 11.7 %fusion.6 = f32[512,6144]{1,0:T(8,128)} fusion(bf16[1536,6144]{1,0:T(8,128)(2,1)} %param.9, bf16[768,768]{1,0:T(8,128)(2,1)S(1)} %bitcast.42, s32[512]{0:T(512)S(1)} %copy-done.7), kind=kOutput, calls=%fused_computation.11 | convolution fusion | flops 5436604416 | bytes 23201792 | tf_op jit(solution)/shard_map/dot_general | solution.py:154
  209.9 12.8 %add_convert_fusion = bf16[512,6144]{1,0:T(8,128)(2,1)} fusion(f32[512,6144]{1,0:T(8,128)} %fusion.6, bf16[1536,6144]{1,0:T(8,128)(2,1)} %param.9, bf16[768,768]{1,0:T(8,128)(2,1)} %bitcast.17, s32[512]{0:T(512)S(1)} %copy-done.7), kind=kOutput, calls=%fused_computation.4 | convolution fusion | flops 5442895872 | bytes 29493248 | tf_op jit(solution)/shard_map/dot_general | solution.py:149
  222.7 62.7 %reduce-scatter.2.cloned.1.call-done = bf16[512,1536]{1,0:T(8,128)(2,1)} async-done(((bf16[512,6144]{1,0:T(8,128)(2,1)}), bf16[512,1536]{1,0:T(8,128)(2,1)}) %reduce-scatter.2.cloned.1.call-update) | async-done | bytes 1572880 | tf_op jit(solution)/shard_map/reduce_scatter | solution.py:156
  (32 shorter events, 7.9 us)
Async XLA Ops:
  6.5 13.7 %copy-start.1 = (bf16[512,1536]{1,0:T(8,128)(2,1)S(1)}, bf16[512,1536]{1,0:T(8,128)(2,1)}, u32[]{:S(2)}) copy-start(bf16[512,1536]{1,0:T(8,128)(2,1)} %param.5) | copy-start | bytes 4718596
  6.5 13.7 %copy-start.2 = (bf16[512,1536]{1,0:T(8,128)(2,1)S(1)}, bf16[512,1536]{1,0:T(8,128)(2,1)}, u32[]{:S(2)}) copy-start(bf16[512,1536]{1,0:T(8,128)(2,1)} %param.6) | copy-start | bytes 4718596
  8.2 17.3 %all-to-all-start.2 = ((s32[32,1,8]{2,1,0:T(1,128)}), s32[32,1,8]{2,1,0:T(1,128)S(1)}, u32[]{:S(2)}, u32[]{:S(2)}) async-start(s32[32,1,8]{2,1,0:T(1,128)} %bitcast.6), calls=%async_computation.2 | async-start | bytes 32768 | tf_op jit(solution)/shard_map/all_to_all | solution.py:101
  17.8 3.7 %copy-start.6 = (s32[512]{0:T(512)}, s32[512]{0:T(512)S(1)}, u32[]{:S(2)}) copy-start(s32[512]{0:T(512)S(1)} %multiply_add_fusion) | copy-start | bytes 6148
  25.5 0.6 copy-start.5
  26.1 51.3 %all-to-all-start.1 = ((bf16[32,24,2304]{2,1,0:T(8,128)(2,1)}), bf16[32,24,2304]{2,1,0:T(8,128)(2,1)S(1)}, u32[]{:S(2)}, u32[]{:S(2)}) async-start(bf16[32,24,2304]{2,1,0:T(8,128)(2,1)} %bitcast.39), calls=%async_computation.1 | async-start | bytes 7077888 | tf_op jit(solution)/shard_map/all_to_all | solution.py:120
  77.4 1.8 copy-start
  79.2 50.9 %all-to-all-start = ((bf16[32,24,2304]{2,1,0:T(8,128)(2,1)}), bf16[32,24,2304]{2,1,0:T(8,128)(2,1)}, u32[]{:S(2)}, u32[]{:S(2)}) async-start(bf16[32,24,2304]{2,1,0:T(8,128)(2,1)} %bitcast.38), calls=%async_computation | async-start | bytes 7077888 | tf_op jit(solution)/shard_map/all_to_all | solution.py:120
  101.5 8.0 %copy-start.4 = (bf16[768,768]{0,1:T(8,128)(2,1)S(1)}, bf16[768,768]{0,1:T(8,128)(2,1)}, u32[]{:S(2)}) copy-start(bf16[768,768]{0,1:T(8,128)(2,1)} %copy.49) | copy-start | bytes 3538948
  138.4 33.7 %all-to-all-start.3 = ((bf16[32,24,768]{2,1,0:T(8,128)(2,1)}), bf16[32,24,768]{2,1,0:T(8,128)(2,1)}, u32[]{:S(2)}, u32[]{:S(2)}) async-start(bf16[32,24,768]{2,1,0:T(8,128)(2,1)} %reshape.228), calls=%async_computation.3 | async-start | bytes 2359296 | tf_op jit(solution)/shard_map/all_to_all | solution.py:123
  145.9 139.6 %reduce-scatter.2.cloned.1.call-start = ((), (), s32[]{:S(2)}) async-start(), calls=%async_computation.6 | async-start | bytes 7864320 | tf_op jit(solution)/shard_map/reduce_scatter | solution.py:156
  152.4 8.0 %copy-start.3 = (bf16[768,768]{0,1:T(8,128)(2,1)S(1)}, bf16[768,768]{0,1:T(8,128)(2,1)}, u32[]{:S(2)}) copy-start(bf16[768,768]{0,1:T(8,128)(2,1)} %copy.59) | copy-start | bytes 3538948
  170.7 27.6 %copy-start.7 = (s32[512]{0:T(512)S(1)}, s32[512]{0:T(512)}, u32[]{:S(2)}) copy-start(s32[512]{0:T(512)} %copy-done.6) | copy-start | bytes 6148
Sparse Core Ops, SparseCore 0:
  222.9 62.5 reduce-scatter.1

commit v4 on v3

--- a/solution.py
+++ b/solution.py
@@ -150,6 +150,8 @@
             partial_value = term if partial_value is None else partial_value + term
         prev_cols = cols
     returned = lax.all_to_all(back, "seq", 0, 0, tiled=True)
+    if partial_value is not None:
+        returned, partial_value = lax.optimization_barrier((returned, partial_value))
     own_rows = permute(to_token, returned.reshape(slots, part))
     term = jnp.dot(own_rows, w_out[prev_cols], preferred_element_type=jnp.float32)
     partial_value = term if partial_value is None else partial_value + term

time: 293 us -> 282 us (0.962)
  blocking collectives: 26.1 us -> 0 us
  starting transfers between devices: 30.7 us -> 38.5 us
  waiting for transfers between devices: 106 us -> 112 us
    all_to_all x1 -> x0, blocking collectives: 26.1 us -> none  [body(): returned = lax.all_to_all(back, 'seq', 0, 0, tiled=True)]
    all_to_all x0 -> x1, starting transfers between devices: none -> 7.5 us  [body(): returned = lax.all_to_all(back, 'seq', 0, 0, tiled=True)]
    all_to_all x0 -> x1, waiting for transfers between devices: none -> 6.26 us  [body(): returned = lax.all_to_all(back, 'seq', 0, 0, tiled=True)]
  transfers between devices with their start and end apart: 5 -> 6, of which waited for: 3 -> 4; matrix products, arithmetic and copies ran while one was open for 27% -> 33% of each run, Pallas kernels for 0% -> 0%
where the time goes in v4:
time: 282 us; the launch traced here: 281 us
  waiting for transfers between devices  112 us (40%)
  matrix products  64.8 us (23%)
  starting transfers between devices  38.5 us (14%)
  local copies, waits for them, and re-layouts  32.1 us (11%)
  other arithmetic  20.2 us (7%)
  between operations  13.6 us (5%)
    reduce_scatter x1, waiting for transfers between devices, body(): lax.psum_scatter(partial_value.astype(jnp.bfloat16), 'head', scatter_dime...  62.7 us
    all_to_all x2, waiting for transfers between devices, body(): lax.all_to_all(outgoing, 'seq', 0, 0, tiled=True).reshape(slots, 3 * part)  42.9 us
    dot_general x2, matrix products, body(): jnp.einsum('hqk,khd->qhd', weights, incoming[:, 2 * part:].reshape(head_s...  18.1 us
    reduce_sum x2, other arithmetic, body(): totals = jnp.sum(exp_scores, axis=-1)  16.1 us
    all_to_all x2, starting transfers between devices, body(): lax.all_to_all(outgoing, 'seq', 0, 0, tiled=True).reshape(slots, 3 * part)  14.6 us
    dot_general x2, matrix products, body(): jnp.einsum('qhd,khd->hqk', incoming[:, :part].reshape(head_shape), incomi...  12.8 us
    dot_general x1, matrix products, body(): jnp.dot(own_rows, w_out[prev_cols], preferred_element_type=jnp.float32)  12.5 us
    dot_general x1, matrix products, body(): jnp.dot(own_rows, w_out[done_cols], preferred_element_type=jnp.float32)  11.9 us
  transfers between devices with their start and end apart: 6, of which 4 were waited for; matrix products, arithmetic and copies ran while one was open for 33% of the time, Pallas kernels for 0%

profile of v4, /device:TPU:1, one launch (start us, length us, event | category | flops | bytes accessed | tf_op | source)
XLA Modules:
  0.0 281.0 jit_solution(12995412079860085500)
XLA Ops:
  8.2 8.6 %all-to-all-start.2 = ((s32[32,1,8]{2,1,0:T(1,128)}), s32[32,1,8]{2,1,0:T(1,128)S(1)}, u32[]{:S(2)}, u32[]{:S(2)}) async-start(s32[32,1,8]{2,1,0:T(1,128)} %bitcast.6), calls=%async_computation.2 | async-start | bytes 32768 | tf_op jit(solution)/shard_map/all_to_all | solution.py:101
  17.9 2.4 fusion.58
  20.2 1.4 fusion.56
  21.6 3.9 %convolution_convert_fusion = bf16[768,2304]{1,0:T(8,128)(2,1)} fusion(bf16[512,768]{1,0:T(8,128)(2,1)S(1)} %get-tuple-element.27, bf16[512,768]{1,0:T(8,128)(2,1)S(1)} %get-tuple-element.36, bf16[512,768]{1,0:T(8,128)(2,1)S(1)} %get-tuple-element.23, s32[512]{0:T(512)S(1)} %multiply_add_fusion), kind=kOutput, calls=%fused_computation.19 | convolution fusion | flops 1821179904 | bytes 5900288 | tf_op jit(solution)/shard_map/dot_general | solution.py:71
  26.1 7.4 %all-to-all-start.1 = ((bf16[32,24,2304]{2,1,0:T(8,128)(2,1)}), bf16[32,24,2304]{2,1,0:T(8,128)(2,1)S(1)}, u32[]{:S(2)}, u32[]{:S(2)}) async-start(bf16[32,24,2304]{2,1,0:T(8,128)(2,1)} %bitcast.39), calls=%async_computation.1 | async-start | bytes 7077888 | tf_op jit(solution)/shard_map/all_to_all | solution.py:120
  33.5 5.5 %convolution_convert_fusion.1 = bf16[768,2304]{1,0:T(8,128)(2,1)} fusion(bf16[512,768]{1,0:T(8,128)(2,1)} %get-tuple-element.28, bf16[512,768]{1,0:T(8,128)(2,1)} %get-tuple-element.35, bf16[512,768]{1,0:T(8,128)(2,1)} %get-tuple-element.24, s32[512]{0:T(512)} %copy-done.6), kind=kOutput, calls=%fused_computation.20 | convolution fusion | flops 1821179904 | bytes 5900288 | tf_op jit(solution)/shard_map/dot_general | solution.py:71
  42.7 34.7 %all-to-all-done.1 = bf16[32,24,2304]{2,1,0:T(8,128)(2,1)S(1)} async-done(((bf16[32,24,2304]{2,1,0:T(8,128)(2,1)}), bf16[32,24,2304]{2,1,0:T(8,128)(2,1)S(1)}, u32[]{:S(2)}, u32[]{:S(2)}) %all-to-all-start.1) | async-done | bytes 3538976 | tf_op jit(solution)/shard_map/all_to_all | solution.py:120
  77.4 1.7 copy-done
  79.2 7.2 %all-to-all-start = ((bf16[32,24,2304]{2,1,0:T(8,128)(2,1)}), bf16[32,24,2304]{2,1,0:T(8,128)(2,1)}, u32[]{:S(2)}, u32[]{:S(2)}) async-start(bf16[32,24,2304]{2,1,0:T(8,128)(2,1)} %bitcast.38), calls=%async_computation | async-start | bytes 7077888 | tf_op jit(solution)/shard_map/all_to_all | solution.py:120
  86.8 3.6 %fusion.55 = (bf16[768,768]{1,0:T(8,128)(2,1)}, bf16[768,768]{1,0:T(8,128)(2,1)S(1)}, bf16[768,768]{1,0:T(8,128)(2,1)}) fusion(bf16[768,2304]{1,0:T(8,128)(2,1)} %bitcast.33), kind=kLoop, calls=%fused_computation.70 | loop fusion | bytes 7077888 | tf_op jit(solution)/shard_map/slice | solution.py:130
  91.1 1.6 copy.54
  92.7 2.4 copy.49
  95.1 6.4 %fusion = (f32[6,768]{1,0:T(8,128)S(1)}, f32[6,768,768]{1,2,0:T(8,128)}) fusion(pred[768,768]{0,1:T(8,128)(4,1)S(1)} %fusion.31, bf16[768,6,128]{0,2,1:T(8,128)(2,1)S(1)} %bitcast.36, bf16[768,6,128]{0,2,1:T(8,128)(2,1)S(1)} %bitcast.37), kind=kOutput, calls=%fused_computation.5 | convolution fusion | flops 916581888 | bytes 17123328 | tf_op jit(solution)/shard_map/qhd,khd->hqk/dot_general | solution.py:127
  101.5 8.0 %fusion.2 = f32[6,768]{1,0:T(8,128)S(1)} fusion(f32[6,768,768]{1,2,0:T(8,128)} %get-tuple-element.32, f32[6,768]{1,0:T(8,128)S(1)} %get-tuple-element.31, pred[768,768]{0,1:T(8,128)(4,1)S(1)} %fusion.31), kind=kLoop, calls=%fused_computation.7 | loop fusion | flops 14151168 | bytes 14782464 | tf_op jit(solution)/shard_map/reduce_sum | solution.py:136
  109.5 9.1 %fusion.29 = bf16[768,6,128]{0,2,1:T(8,128)(2,1)S(1)} fusion(bf16[768,6,128]{0,2,1:T(8,128)(2,1)S(1)} %bitcast.42, f32[6,768,768]{1,2,0:T(8,128)} %get-tuple-element.32, f32[6,768]{1,0:T(8,128)S(1)} %get-tuple-element.31, pred[768,768]{0,1:T(8,128)(4,1)S(1)} %fusion.31, f32[768,6]{0,1:T(8,128)S(1)} %bitcast.45), kind=kOutput, calls=%fused_computation.34 | convolution fusion | flops 921305088 | bytes 17141760 | tf_op jit(solution)/shard_map/hqk,khd->qhd/dot_general | solution.py:138
  118.6 1.1 copy.58
  119.7 2.2 reshape.228
  121.9 8.2 %all-to-all-done = bf16[32,24,2304]{2,1,0:T(8,128)(2,1)} async-done(((bf16[32,24,2304]{2,1,0:T(8,128)(2,1)}), bf16[32,24,2304]{2,1,0:T(8,128)(2,1)}, u32[]{:S(2)}, u32[]{:S(2)}) %all-to-all-start) | async-done | bytes 3538976 | tf_op jit(solution)/shard_map/all_to_all | solution.py:120
  130.1 3.6 %fusion.54 = (bf16[768,768]{1,0:T(8,128)(2,1)}, bf16[768,768]{1,0:T(8,128)(2,1)S(1)}, bf16[768,768]{1,0:T(8,128)(2,1)}) fusion(bf16[768,2304]{1,0:T(8,128)(2,1)} %bitcast.2), kind=kLoop, calls=%fused_computation.69 | loop fusion | bytes 7077888 | tf_op jit(solution)/shard_map/slice | solution.py:130
  134.4 1.6 copy.61
  136.0 2.4 copy.59
  138.4 7.6 %all-to-all-start.3 = ((bf16[32,24,768]{2,1,0:T(8,128)(2,1)}), bf16[32,24,768]{2,1,0:T(8,128)(2,1)}, u32[]{:S(2)}, u32[]{:S(2)}) async-start(bf16[32,24,768]{2,1,0:T(8,128)(2,1)} %reshape.228), calls=%async_computation.3 | async-start | bytes 2359296 | tf_op jit(solution)/shard_map/all_to_all | solution.py:123
  146.0 6.4 %fusion.1 = (f32[6,768]{1,0:T(8,128)S(1)}, f32[6,768,768]{1,2,0:T(8,128)}) fusion(pred[768,768]{0,1:T(8,128)(4,1)S(1)} %fusion.31, bf16[768,6,128]{0,2,1:T(8,128)(2,1)S(1)} %bitcast.34, bf16[768,6,128]{0,2,1:T(8,128)(2,1)S(1)} %bitcast.35), kind=kOutput, calls=%fused_computation.6 | convolution fusion | flops 916581888 | bytes 17123328 | tf_op jit(solution)/shard_map/qhd,khd->hqk/dot_general | solution.py:127
  152.4 8.0 %fusion.4 = f32[6,768]{1,0:T(8,128)S(1)} fusion(f32[6,768,768]{1,2,0:T(8,128)} %get-tuple-element.34, f32[6,768]{1,0:T(8,128)S(1)} %get-tuple-element.33, pred[768,768]{0,1:T(8,128)(4,1)S(1)} %fusion.31), kind=kLoop, calls=%fused_computation.9 | loop fusion | flops 14151168 | bytes 14782464 | tf_op jit(solution)/shard_map/reduce_sum | solution.py:136
  160.4 9.1 %fusion.28 = bf16[768,6,128]{0,2,1:T(8,128)(2,1)S(1)} fusion(bf16[768,6,128]{0,2,1:T(8,128)(2,1)S(1)} %bitcast.40, f32[6,768,768]{1,2,0:T(8,128)} %get-tuple-element.34, f32[6,768]{1,0:T(8,128)S(1)} %get-tuple-element.33, pred[768,768]{0,1:T(8,128)(4,1)S(1)} %fusion.31, f32[768,6]{0,1:T(8,128)S(1)} %bitcast.44), kind=kOutput, calls=%fused_computation.32 | convolution fusion | flops 921305088 | bytes 17141760 | tf_op jit(solution)/shard_map/hqk,khd->qhd/dot_general | solution.py:138
  169.5 1.1 copy.65
  170.7 2.2 reshape.232
  172.9 7.5 %all-to-all-start.4 = ((bf16[32,24,768]{2,1,0:T(8,128)(2,1)}), bf16[32,24,768]{2,1,0:T(8,128)(2,1)S(1)}, u32[]{:S(2)}, u32[]{:S(2)}) async-start(bf16[32,24,768]{2,1,0:T(8,128)(2,1)} %reshape.232), calls=%async_computation.4 | async-start | bytes 2359296 | tf_op jit(solution)/shard_map/all_to_all | solution.py:152
  180.7 11.9 %fusion.8 = f32[512,6144]{1,0:T(8,128)} fusion(bf16[1536,6144]{1,0:T(8,128)(2,1)} %param.9, bf16[768,768]{1,0:T(8,128)(2,1)} %bitcast.17, s32[512]{0:T(512)S(1)} %copy-done.7), kind=kOutput, calls=%fused_computation.13 | convolution fusion | flops 5436604416 | bytes 23201792 | tf_op jit(solution)/shard_map/dot_general | solution.py:149
  192.7 6.3 %all-to-all-done.4 = bf16[32,24,768]{2,1,0:T(8,128)(2,1)S(1)} async-done(((bf16[32,24,768]{2,1,0:T(8,128)(2,1)}), bf16[32,24,768]{2,1,0:T(8,128)(2,1)S(1)}, u32[]{:S(2)}, u32[]{:S(2)}) %all-to-all-start.4) | async-done | bytes 1179680 | tf_op jit(solution)/shard_map/all_to_all | solution.py:152
  198.9 12.5 %add_convert_fusion = bf16[512,6144]{1,0:T(8,128)(2,1)} fusion(f32[512,6144]{1,0:T(8,128)} %fusion.8, bf16[1536,6144]{1,0:T(8,128)(2,1)} %param.9, bf16[768,768]{1,0:T(8,128)(2,1)S(1)} %bitcast.41, s32[512]{0:T(512)S(1)} %copy-done.7), kind=kOutput, calls=%fused_computation.4 | convolution fusion | flops 5442895872 | bytes 29493248 | tf_op jit(solution)/shard_map/dot_general | solution.py:156
  211.5 62.7 %reduce-scatter.2.cloned.1.call-done = bf16[512,1536]{1,0:T(8,128)(2,1)} async-done(((bf16[512,6144]{1,0:T(8,128)(2,1)}), bf16[512,1536]{1,0:T(8,128)(2,1)}) %reduce-scatter.2.cloned.1.call-update) | async-done | bytes 1572880 | tf_op jit(solution)/shard_map/reduce_scatter | solution.py:158
  (33 shorter events, 9.1 us)
Async XLA Ops:
  6.5 13.7 %copy-start.1 = (bf16[512,1536]{1,0:T(8,128)(2,1)S(1)}, bf16[512,1536]{1,0:T(8,128)(2,1)}, u32[]{:S(2)}) copy-start(bf16[512,1536]{1,0:T(8,128)(2,1)} %param.5) | copy-start | bytes 4718596
  6.5 13.7 %copy-start.2 = (bf16[512,1536]{1,0:T(8,128)(2,1)S(1)}, bf16[512,1536]{1,0:T(8,128)(2,1)}, u32[]{:S(2)}) copy-start(bf16[512,1536]{1,0:T(8,128)(2,1)} %param.6) | copy-start | bytes 4718596
  8.2 17.3 %all-to-all-start.2 = ((s32[32,1,8]{2,1,0:T(1,128)}), s32[32,1,8]{2,1,0:T(1,128)S(1)}, u32[]{:S(2)}, u32[]{:S(2)}) async-start(s32[32,1,8]{2,1,0:T(1,128)} %bitcast.6), calls=%async_computation.2 | async-start | bytes 32768 | tf_op jit(solution)/shard_map/all_to_all | solution.py:101
  17.8 3.7 %copy-start.6 = (s32[512]{0:T(512)}, s32[512]{0:T(512)S(1)}, u32[]{:S(2)}) copy-start(s32[512]{0:T(512)S(1)} %multiply_add_fusion) | copy-start | bytes 6148
  25.5 0.6 copy-start.5
  26.1 51.3 %all-to-all-start.1 = ((bf16[32,24,2304]{2,1,0:T(8,128)(2,1)}), bf16[32,24,2304]{2,1,0:T(8,128)(2,1)S(1)}, u32[]{:S(2)}, u32[]{:S(2)}) async-start(bf16[32,24,2304]{2,1,0:T(8,128)(2,1)} %bitcast.39), calls=%async_computation.1 | async-start | bytes 7077888 | tf_op jit(solution)/shard_map/all_to_all | solution.py:120
  77.4 1.7 copy-start
  79.2 50.9 %all-to-all-start = ((bf16[32,24,2304]{2,1,0:T(8,128)(2,1)}), bf16[32,24,2304]{2,1,0:T(8,128)(2,1)}, u32[]{:S(2)}, u32[]{:S(2)}) async-start(bf16[32,24,2304]{2,1,0:T(8,128)(2,1)} %bitcast.38), calls=%async_computation | async-start | bytes 7077888 | tf_op jit(solution)/shard_map/all_to_all | solution.py:120
  101.5 8.0 %copy-start.4 = (bf16[768,768]{0,1:T(8,128)(2,1)S(1)}, bf16[768,768]{0,1:T(8,128)(2,1)}, u32[]{:S(2)}) copy-start(bf16[768,768]{0,1:T(8,128)(2,1)} %copy.49) | copy-start | bytes 3538948
  138.4 34.5 %all-to-all-start.3 = ((bf16[32,24,768]{2,1,0:T(8,128)(2,1)}), bf16[32,24,768]{2,1,0:T(8,128)(2,1)}, u32[]{:S(2)}, u32[]{:S(2)}) async-start(bf16[32,24,768]{2,1,0:T(8,128)(2,1)} %reshape.228), calls=%async_computation.3 | async-start | bytes 2359296 | tf_op jit(solution)/shard_map/all_to_all | solution.py:123
  152.4 8.0 %copy-start.3 = (bf16[768,768]{0,1:T(8,128)(2,1)S(1)}, bf16[768,768]{0,1:T(8,128)(2,1)}, u32[]{:S(2)}) copy-start(bf16[768,768]{0,1:T(8,128)(2,1)} %copy.59) | copy-start | bytes 3538948
  170.7 10.1 %copy-start.7 = (s32[512]{0:T(512)S(1)}, s32[512]{0:T(512)}, u32[]{:S(2)}) copy-start(s32[512]{0:T(512)} %copy-done.6) | copy-start | bytes 6148
  172.9 26.0 %all-to-all-start.4 = ((bf16[32,24,768]{2,1,0:T(8,128)(2,1)}), bf16[32,24,768]{2,1,0:T(8,128)(2,1)S(1)}, u32[]{:S(2)}, u32[]{:S(2)}) async-start(bf16[32,24,768]{2,1,0:T(8,128)(2,1)} %reshape.232), calls=%async_computation.4 | async-start | bytes 2359296 | tf_op jit(solution)/shard_map/all_to_all | solution.py:152
  180.4 93.8 %reduce-scatter.2.cloned.1.call-start = ((), (), s32[]{:S(2)}) async-start(), calls=%async_computation.6 | async-start | bytes 7864320 | tf_op jit(solution)/shard_map/reduce_scatter | solution.py:158
Sparse Core Ops, SparseCore 0:
  211.6 62.5 reduce-scatter.1

commit v5 on v4

--- a/solution.py
+++ b/solution.py
@@ -94,30 +94,28 @@
     to_token = one_hot(dest, slots)
     to_slot = to_token.T
 
-    counts = jnp.sum(
-        (cluster[:, None] == jnp.arange(NCLUST, dtype=jnp.int32)[None, :]).astype(jnp.int32),
-        axis=0,
-    ).reshape(seq_count, cl_dev)
-    count_in = lax.all_to_all(counts, "seq", 0, 0, tiled=True)
+    tag = jnp.zeros((tokens, HD), jnp.bfloat16).at[:, 0].set(
+        (cluster % cl_dev + 1).astype(jnp.bfloat16)
+    )
 
-    ends = jnp.cumsum(count_in, axis=1)
-    j = jnp.arange(rows, dtype=jnp.int32)
-    c_of = jnp.sum((ends[:, None, :] <= j[None, :, None]).astype(jnp.int32), axis=2)
-    row_cluster = c_of.reshape(slots)
-    valid = row_cluster < cl_dev
     flat = jnp.arange(slots, dtype=jnp.int32)
-    allowed = (
-        (row_cluster[:, None] == row_cluster[None, :])
-        & valid[None, :]
-        & (flat[None, :] <= flat[:, None])
-    ) | (flat[None, :] == flat[:, None])
 
     partial_value = None
     for k in range(split):
         cols = slice(k * part, (k + 1) * part)
-        packed = jnp.concatenate([queries[:, cols], keys[:, cols], values[:, cols]], axis=1)
-        outgoing = permute(to_slot, packed).reshape(seq_count, rows, 3 * part)
-        incoming = lax.all_to_all(outgoing, "seq", 0, 0, tiled=True).reshape(slots, 3 * part)
+        pieces = [queries[:, cols], keys[:, cols], values[:, cols]] + ([tag] if k == 0 else [])
+        packed = jnp.concatenate(pieces, axis=1)
+        width = packed.shape[1]
+        outgoing = permute(to_slot, packed).reshape(seq_count, rows, width)
+        incoming = lax.all_to_all(outgoing, "seq", 0, 0, tiled=True).reshape(slots, width)
+        if k == 0:
+            row_cluster = incoming[:, 3 * part].astype(jnp.int32) - 1
+            valid = row_cluster >= 0
+            allowed = (
+                (row_cluster[:, None] == row_cluster[None, :])
+                & valid[None, :]
+                & (flat[None, :] <= flat[:, None])
+            ) | (flat[None, :] == flat[:, None])
         if k > 0:
             incoming, back = lax.optimization_barrier((incoming, back))
             returned_prev = lax.all_to_all(back, "seq", 0, 0, tiled=True)
@@ -138,7 +136,7 @@
         attended = jnp.einsum(
             "hqk,khd->qhd",
             weights,
-            incoming[:, 2 * part :].reshape(head_shape),
+            incoming[:, 2 * part : 3 * part].reshape(head_shape),
             preferred_element_type=jnp.float32,
         )
         attended = attended / totals.T[:, :, None]

time: 282 us -> 276 us (0.979)
  starting transfers between devices: 38.5 us -> 30.9 us
  waiting for transfers between devices: 112 us -> 118 us
  local copies, waits for them, and re-layouts: 32.1 us -> 27.7 us
    all_to_all x3 -> x2, starting transfers between devices: 23.1 us -> 16.1 us  [body(): lax.all_to_all(outgoing, 'seq', 0, 0, tiled=True).reshape(slots, width)]
    all_to_all x3 -> x2, waiting for transfers between devices: 42.9 us -> 49.2 us  [body(): lax.all_to_all(outgoing, 'seq', 0, 0, tiled=True).reshape(slots, width)]
  transfers between devices with their start and end apart: 6 -> 5, of which waited for: 4 -> 4; matrix products, arithmetic and copies ran while one was open for 33% -> 29% of each run, Pallas kernels for 0% -> 0%
where the time goes in v5:
time: 276 us; the launch traced here: 275 us
  waiting for transfers between devices  118 us (43%)
  matrix products  63.9 us (23%)
  starting transfers between devices  30.9 us (11%)
  local copies, waits for them, and re-layouts  27.7 us (10%)
  other arithmetic  21 us (8%)
  between operations  13.6 us (5%)
    reduce_scatter x1, waiting for transfers between devices, body(): lax.psum_scatter(partial_value.astype(jnp.bfloat16), 'head', scatter_dime...  62.7 us
    all_to_all x2, waiting for transfers between devices, body(): lax.all_to_all(outgoing, 'seq', 0, 0, tiled=True).reshape(slots, width)  49.2 us
    dot_general x2, matrix products, body(): jnp.einsum('hqk,khd->qhd', weights, incoming[:, 2 * part:3 * part].reshap...  18.1 us
    reduce_sum x2, other arithmetic, body(): totals = jnp.sum(exp_scores, axis=-1)  16.1 us
    all_to_all x2, starting transfers between devices, body(): lax.all_to_all(outgoing, 'seq', 0, 0, tiled=True).reshape(slots, width)  16.1 us
    dot_general x2, matrix products, body(): jnp.einsum('qhd,khd->hqk', incoming[:, :part].reshape(head_shape), incomi...  12.9 us
    dot_general x1, matrix products, body(): jnp.dot(own_rows, w_out[prev_cols], preferred_element_type=jnp.float32)  12.5 us
    dot_general x1, matrix products, body(): jnp.dot(own_rows, w_out[done_cols], preferred_element_type=jnp.float32)  12.3 us
  transfers between devices with their start and end apart: 5, of which 4 were waited for; matrix products, arithmetic and copies ran while one was open for 29% of the time, Pallas kernels for 0%

profile of v5, /device:TPU:1, one launch (start us, length us, event | category | flops | bytes accessed | tf_op | source)
XLA Modules:
  0.0 275.2 jit_solution(14577094408850357867)
XLA Ops:
  8.5 2.6 fusion.69
  11.1 1.3 broadcast_select_fusion
  12.7 1.5 fusion.67
  14.2 4.2 %convolution_convert_fusion = bf16[768,2432]{1,0:T(8,128)(2,1)} fusion(bf16[512,1]{1,0:T(8,128)(2,1)S(1)} %copy.57, bf16[512,768]{1,0:T(8,128)(2,1)S(1)} %copy-done.7, bf16[512,768]{1,0:T(8,128)(2,1)S(1)} %get-tuple-element.48, bf16[512,768]{1,0:T(8,128)(2,1)S(1)} %get-tuple-element.35, s32[512]{0:T(512)S(1)} %multiply_add_fusion), kind=kOutput, calls=%fused_computation.19 | convolution fusion | flops 1927315456 | bytes 6097920 | tf_op jit(solution)/shard_map/dot_general | solution.py:71
  18.4 8.8 %all-to-all-start.1 = ((bf16[32,24,2432]{2,1,0:T(8,128)(2,1)}), bf16[32,24,2432]{2,1,0:T(8,128)(2,1)}, u32[]{:S(2)}, u32[]{:S(2)}) async-start(bf16[32,24,2432]{2,1,0:T(8,128)(2,1)} %bitcast.37), calls=%async_computation.1 | async-start | bytes 7471104 | tf_op jit(solution)/shard_map/all_to_all | solution.py:110
  27.1 3.9 %convolution_convert_fusion.1 = bf16[768,2304]{1,0:T(8,128)(2,1)} fusion(bf16[512,768]{1,0:T(8,128)(2,1)S(1)} %copy-done.6, bf16[512,768]{1,0:T(8,128)(2,1)S(1)} %copy-done.5, bf16[512,768]{1,0:T(8,128)(2,1)S(1)} %copy-done.4, s32[512]{0:T(512)S(1)} %multiply_add_fusion), kind=kOutput, calls=%fused_computation.20 | convolution fusion | flops 1821179904 | bytes 5900288 | tf_op jit(solution)/shard_map/dot_general | solution.py:71
  31.0 42.2 %all-to-all-done.1 = bf16[32,24,2432]{2,1,0:T(8,128)(2,1)} async-done(((bf16[32,24,2432]{2,1,0:T(8,128)(2,1)}), bf16[32,24,2432]{2,1,0:T(8,128)(2,1)}, u32[]{:S(2)}, u32[]{:S(2)}) %all-to-all-start.1) | async-done | bytes 3735584 | tf_op jit(solution)/shard_map/all_to_all | solution.py:110
  73.2 7.3 %all-to-all-start = ((bf16[32,24,2304]{2,1,0:T(8,128)(2,1)}), bf16[32,24,2304]{2,1,0:T(8,128)(2,1)}, u32[]{:S(2)}, u32[]{:S(2)}) async-start(bf16[32,24,2304]{2,1,0:T(8,128)(2,1)} %bitcast.1), calls=%async_computation | async-start | bytes 7077888 | tf_op jit(solution)/shard_map/all_to_all | solution.py:110
  80.5 1.1 add_reduce_fusion
  81.6 3.6 %fusion.65 = (bf16[768,768]{1,0:T(8,128)(2,1)}, bf16[768,768]{1,0:T(8,128)(2,1)S(1)}, bf16[768,768]{1,0:T(8,128)(2,1)}) fusion(bf16[768,2432]{1,0:T(8,128)(2,1)} %bitcast.5), kind=kLoop, calls=%fused_computation.82 | loop fusion | bytes 7077888 | tf_op jit(solution)/shard_map/slice | solution.py:128
  85.9 1.6 copy.39
  87.5 2.4 copy.37
  90.3 6.4 %fusion = (f32[6,768]{1,0:T(8,128)S(1)}, f32[6,768,768]{1,2,0:T(8,128)}) fusion(pred[768,768]{0,1:T(8,128)(4,1)S(1)} %fusion.36, bf16[768,6,128]{0,2,1:T(8,128)(2,1)S(1)} %bitcast.34, bf16[768,6,128]{0,2,1:T(8,128)(2,1)S(1)} %bitcast.36), kind=kOutput, calls=%fused_computation.5 | convolution fusion | flops 916581888 | bytes 17123328 | tf_op jit(solution)/shard_map/qhd,khd->hqk/dot_general | solution.py:125
  96.8 8.0 %fusion.2 = f32[6,768]{1,0:T(8,128)S(1)} fusion(f32[6,768,768]{1,2,0:T(8,128)} %get-tuple-element.44, f32[6,768]{1,0:T(8,128)S(1)} %get-tuple-element.43, pred[768,768]{0,1:T(8,128)(4,1)S(1)} %fusion.36), kind=kLoop, calls=%fused_computation.7 | loop fusion | flops 14151168 | bytes 14782464 | tf_op jit(solution)/shard_map/reduce_sum | solution.py:134
  104.8 9.1 %fusion.34 = bf16[768,6,128]{0,2,1:T(8,128)(2,1)S(1)} fusion(bf16[768,6,128]{0,2,1:T(8,128)(2,1)S(1)} %bitcast.40, f32[6,768,768]{1,2,0:T(8,128)} %get-tuple-element.44, f32[6,768]{1,0:T(8,128)S(1)} %get-tuple-element.43, pred[768,768]{0,1:T(8,128)(4,1)S(1)} %fusion.36, f32[768,6]{0,1:T(8,128)S(1)} %bitcast.42), kind=kOutput, calls=%fused_computation.39 | convolution fusion | flops 921305088 | bytes 17141760 | tf_op jit(solution)/shard_map/hqk,khd->qhd/dot_general | solution.py:136
  113.9 1.1 copy.43
  115.1 2.2 reshape.289
  117.3 7.0 %all-to-all-done = bf16[32,24,2304]{2,1,0:T(8,128)(2,1)} async-done(((bf16[32,24,2304]{2,1,0:T(8,128)(2,1)}), bf16[32,24,2304]{2,1,0:T(8,128)(2,1)}, u32[]{:S(2)}, u32[]{:S(2)}) %all-to-all-start) | async-done | bytes 3538976 | tf_op jit(solution)/shard_map/all_to_all | solution.py:110
  124.3 3.6 %fusion.66 = (bf16[768,768]{1,0:T(8,128)(2,1)}, bf16[768,768]{1,0:T(8,128)(2,1)S(1)}, bf16[768,768]{1,0:T(8,128)(2,1)}) fusion(bf16[768,2304]{1,0:T(8,128)(2,1)} %bitcast.2), kind=kLoop, calls=%fused_computation.83 | loop fusion | bytes 7077888 | tf_op jit(solution)/shard_map/slice | solution.py:128
  128.5 1.6 copy.46
  130.1 2.6 copy.44
  132.8 7.3 %all-to-all-start.2 = ((bf16[32,24,768]{2,1,0:T(8,128)(2,1)}), bf16[32,24,768]{2,1,0:T(8,128)(2,1)}, u32[]{:S(2)}, u32[]{:S(2)}) async-start(bf16[32,24,768]{2,1,0:T(8,128)(2,1)} %reshape.289), calls=%async_computation.2 | async-start | bytes 2359296 | tf_op jit(solution)/shard_map/all_to_all | solution.py:121
  140.1 6.4 %fusion.1 = (f32[6,768]{1,0:T(8,128)S(1)}, f32[6,768,768]{1,2,0:T(8,128)}) fusion(pred[768,768]{0,1:T(8,128)(4,1)S(1)} %fusion.36, bf16[768,6,128]{0,2,1:T(8,128)(2,1)S(1)} %bitcast.33, bf16[768,6,128]{0,2,1:T(8,128)(2,1)S(1)} %bitcast.35), kind=kOutput, calls=%fused_computation.6 | convolution fusion | flops 916581888 | bytes 17123328 | tf_op jit(solution)/shard_map/qhd,khd->hqk/dot_general | solution.py:125
  146.5 8.0 %fusion.4 = f32[6,768]{1,0:T(8,128)S(1)} fusion(f32[6,768,768]{1,2,0:T(8,128)} %get-tuple-element.46, f32[6,768]{1,0:T(8,128)S(1)} %get-tuple-element.45, pred[768,768]{0,1:T(8,128)(4,1)S(1)} %fusion.36), kind=kLoop, calls=%fused_computation.9 | loop fusion | flops 14151168 | bytes 14782464 | tf_op jit(solution)/shard_map/reduce_sum | solution.py:134
  154.6 9.1 %fusion.33 = bf16[768,6,128]{0,2,1:T(8,128)(2,1)S(1)} fusion(bf16[768,6,128]{0,2,1:T(8,128)(2,1)S(1)} %bitcast.38, f32[6,768,768]{1,2,0:T(8,128)} %get-tuple-element.46, f32[6,768]{1,0:T(8,128)S(1)} %get-tuple-element.45, pred[768,768]{0,1:T(8,128)(4,1)S(1)} %fusion.36, f32[768,6]{0,1:T(8,128)S(1)} %bitcast.41), kind=kOutput, calls=%fused_computation.37 | convolution fusion | flops 921305088 | bytes 17141760 | tf_op jit(solution)/shard_map/hqk,khd->qhd/dot_general | solution.py:136
  163.7 1.1 copy.50
  164.8 2.2 reshape.293
  167.1 7.5 %all-to-all-start.3 = ((bf16[32,24,768]{2,1,0:T(8,128)(2,1)}), bf16[32,24,768]{2,1,0:T(8,128)(2,1)S(1)}, u32[]{:S(2)}, u32[]{:S(2)}) async-start(bf16[32,24,768]{2,1,0:T(8,128)(2,1)} %reshape.293), calls=%async_computation.3 | async-start | bytes 2359296 | tf_op jit(solution)/shard_map/all_to_all | solution.py:150
  174.6 12.3 %fusion.8 = f32[512,6144]{1,0:T(8,128)} fusion(bf16[1536,6144]{1,0:T(8,128)(2,1)} %param.11, bf16[768,768]{1,0:T(8,128)(2,1)} %bitcast.16, s32[512]{0:T(512)S(1)} %multiply_add_fusion), kind=kOutput, calls=%fused_computation.13 | convolution fusion | flops 5436604416 | bytes 23201792 | tf_op jit(solution)/shard_map/dot_general | solution.py:147
  186.9 6.1 %all-to-all-done.3 = bf16[32,24,768]{2,1,0:T(8,128)(2,1)S(1)} async-done(((bf16[32,24,768]{2,1,0:T(8,128)(2,1)}), bf16[32,24,768]{2,1,0:T(8,128)(2,1)S(1)}, u32[]{:S(2)}, u32[]{:S(2)}) %all-to-all-start.3) | async-done | bytes 1179680 | tf_op jit(solution)/shard_map/all_to_all | solution.py:150
  193.1 12.5 %add_convert_fusion = bf16[512,6144]{1,0:T(8,128)(2,1)} fusion(f32[512,6144]{1,0:T(8,128)} %fusion.8, bf16[1536,6144]{1,0:T(8,128)(2,1)} %param.11, bf16[768,768]{1,0:T(8,128)(2,1)S(1)} %bitcast.39, s32[512]{0:T(512)S(1)} %multiply_add_fusion), kind=kOutput, calls=%fused_computation.4 | convolution fusion | flops 5442895872 | bytes 29493248 | tf_op jit(solution)/shard_map/dot_general | solution.py:154
  205.6 62.7 %reduce-scatter.2.cloned.1.call-done = bf16[512,1536]{1,0:T(8,128)(2,1)} async-done(((bf16[512,6144]{1,0:T(8,128)(2,1)}), bf16[512,1536]{1,0:T(8,128)(2,1)}) %reduce-scatter.2.cloned.1.call-update) | async-done | bytes 1572880 | tf_op jit(solution)/shard_map/reduce_scatter | solution.py:156
  (28 shorter events, 4.0 us)
Async XLA Ops:
  6.5 6.1 %copy-start = (bf16[512,1536]{1,0:T(8,128)(2,1)S(1)}, bf16[512,1536]{1,0:T(8,128)(2,1)}, u32[]{:S(2)}) copy-start(bf16[512,1536]{1,0:T(8,128)(2,1)} %param.7) | copy-start | bytes 4718596
  6.5 6.1 %copy-start.1 = (bf16[512,1536]{1,0:T(8,128)(2,1)S(1)}, bf16[512,1536]{1,0:T(8,128)(2,1)}, u32[]{:S(2)}) copy-start(bf16[512,1536]{1,0:T(8,128)(2,1)} %param.8) | copy-start | bytes 4718596
  12.7 1.5 copy-start.7
  18.3 8.8 %copy-start.4 = (bf16[512,768]{1,0:T(8,128)(2,1)S(1)}, bf16[512,768]{1,0:T(8,128)(2,1)}, u32[]{:S(2)}) copy-start(bf16[512,768]{1,0:T(8,128)(2,1)} %get-tuple-element.36) | copy-start | bytes 2359300
  18.3 8.8 %copy-start.5 = (bf16[512,768]{1,0:T(8,128)(2,1)S(1)}, bf16[512,768]{1,0:T(8,128)(2,1)}, u32[]{:S(2)}) copy-start(bf16[512,768]{1,0:T(8,128)(2,1)} %get-tuple-element.47) | copy-start | bytes 2359300
  18.4 8.8 %copy-start.6 = (bf16[512,768]{1,0:T(8,128)(2,1)S(1)}, bf16[512,768]{1,0:T(8,128)(2,1)}, u32[]{:S(2)}) copy-start(bf16[512,768]{1,0:T(8,128)(2,1)} %get-tuple-element.40) | copy-start | bytes 2359300
  18.4 54.8 %all-to-all-start.1 = ((bf16[32,24,2432]{2,1,0:T(8,128)(2,1)}), bf16[32,24,2432]{2,1,0:T(8,128)(2,1)}, u32[]{:S(2)}, u32[]{:S(2)}) async-start(bf16[32,24,2432]{2,1,0:T(8,128)(2,1)} %bitcast.37), calls=%async_computation.1 | async-start | bytes 7471104 | tf_op jit(solution)/shard_map/all_to_all | solution.py:110
  73.2 51.1 %all-to-all-start = ((bf16[32,24,2304]{2,1,0:T(8,128)(2,1)}), bf16[32,24,2304]{2,1,0:T(8,128)(2,1)}, u32[]{:S(2)}, u32[]{:S(2)}) async-start(bf16[32,24,2304]{2,1,0:T(8,128)(2,1)} %bitcast.1), calls=%async_computation | async-start | bytes 7077888 | tf_op jit(solution)/shard_map/all_to_all | solution.py:110
  96.8 8.0 %copy-start.3 = (bf16[768,768]{0,1:T(8,128)(2,1)S(1)}, bf16[768,768]{0,1:T(8,128)(2,1)}, u32[]{:S(2)}) copy-start(bf16[768,768]{0,1:T(8,128)(2,1)} %copy.37) | copy-start | bytes 3538948
  132.8 34.3 %all-to-all-start.2 = ((bf16[32,24,768]{2,1,0:T(8,128)(2,1)}), bf16[32,24,768]{2,1,0:T(8,128)(2,1)}, u32[]{:S(2)}, u32[]{:S(2)}) async-start(bf16[32,24,768]{2,1,0:T(8,128)(2,1)} %reshape.289), calls=%async_computation.2 | async-start | bytes 2359296 | tf_op jit(solution)/shard_map/all_to_all | solution.py:121
  146.5 8.0 %copy-start.2 = (bf16[768,768]{0,1:T(8,128)(2,1)S(1)}, bf16[768,768]{0,1:T(8,128)(2,1)}, u32[]{:S(2)}) copy-start(bf16[768,768]{0,1:T(8,128)(2,1)} %copy.44) | copy-start | bytes 3538948
  167.1 26.0 %all-to-all-start.3 = ((bf16[32,24,768]{2,1,0:T(8,128)(2,1)}), bf16[32,24,768]{2,1,0:T(8,128)(2,1)S(1)}, u32[]{:S(2)}, u32[]{:S(2)}) async-start(bf16[32,24,768]{2,1,0:T(8,128)(2,1)} %reshape.293), calls=%async_computation.3 | async-start | bytes 2359296 | tf_op jit(solution)/shard_map/all_to_all | solution.py:150
  174.6 93.8 %reduce-scatter.2.cloned.1.call-start = ((), (), s32[]{:S(2)}) async-start(), calls=%async_computation.5 | async-start | bytes 7864320 | tf_op jit(solution)/shard_map/reduce_scatter | solution.py:156
Sparse Core Ops, SparseCore 0:
  205.8 62.5 reduce-scatter.1

commit v6 on v5

--- a/solution.py
+++ b/solution.py
@@ -79,7 +79,10 @@
     features = queries.shape[1]
     heads_here = features // HD
     split = NSPLIT if heads_here % NSPLIT == 0 else 1
-    part = features // split
+    if split == 2 and heads_here % 3 == 0:
+        bounds = [0, 2 * features // 3, features]
+    else:
+        bounds = [k * (features // split) for k in range(split + 1)]
     rows = OWNER_CAP
     slots = seq_count * rows
     bucket_rows = cl_dev * seq_count * CAP
@@ -102,7 +105,8 @@
 
     partial_value = None
     for k in range(split):
-        cols = slice(k * part, (k + 1) * part)
+        part = bounds[k + 1] - bounds[k]
+        cols = slice(bounds[k], bounds[k + 1])
         pieces = [queries[:, cols], keys[:, cols], values[:, cols]] + ([tag] if k == 0 else [])
         packed = jnp.concatenate(pieces, axis=1)
         width = packed.shape[1]
@@ -143,14 +147,14 @@
         back = attended.astype(jnp.bfloat16).reshape(seq_count, rows, part)
         if k > 0:
             back, returned_prev = lax.optimization_barrier((back, returned_prev))
-            own_rows = permute(to_token, returned_prev.reshape(slots, part))
+            own_rows = permute(to_token, returned_prev.reshape(slots, -1))
             term = jnp.dot(own_rows, w_out[done_cols], preferred_element_type=jnp.float32)
             partial_value = term if partial_value is None else partial_value + term
         prev_cols = cols
     returned = lax.all_to_all(back, "seq", 0, 0, tiled=True)
     if partial_value is not None:
         returned, partial_value = lax.optimization_barrier((returned, partial_value))
-    own_rows = permute(to_token, returned.reshape(slots, part))
+    own_rows = permute(to_token, returned.reshape(slots, -1))
     term = jnp.dot(own_rows, w_out[prev_cols], preferred_element_type=jnp.float32)
     partial_value = term if partial_value is None else partial_value + term
     summed = lax.psum_scatter(

time: 276 us -> 284 us (1.029)
  waiting for transfers between devices: 118 us -> 135 us
  other arithmetic: 21 us -> 16.5 us
  matrix products: 63.9 us -> 60.9 us
    all_to_all x1, waiting for transfers between devices: 0.01 us -> 13.5 us  [body(): returned_prev = lax.all_to_all(back, 'seq', 0, 0, tiled=True)]
    all_to_all x1, waiting for transfers between devices: 6.15 us -> 0.01 us  [body(): returned = lax.all_to_all(back, 'seq', 0, 0, tiled=True)]
    all_to_all x2, waiting for transfers between devices: 49.2 us -> 55.3 us  [body(): lax.all_to_all(outgoing, 'seq', 0, 0, tiled=True).reshape(slots, width)]
    dot_general x2, matrix products: 18.1 us -> 13.2 us  [body(): jnp.einsum('hqk,khd->qhd', weights, incoming[:, 2 * part:3 * part].reshap...]
    reduce_sum x2, other arithmetic: 16.1 us -> 12.3 us  [body(): totals = jnp.sum(exp_scores, axis=-1)]
    reduce_scatter x1, waiting for transfers between devices: 62.7 us -> 66.4 us  [body(): lax.psum_scatter(partial_value.astype(jnp.bfloat16), 'head', scatter_dime...]
  transfers between devices with their start and end apart: 5 -> 5, of which waited for: 4 -> 3; matrix products, arithmetic and copies ran while one was open for 29% -> 28% of each run, Pallas kernels for 0% -> 0%
where the time goes in v6:
time: 284 us; the launch traced here: 283 us
  waiting for transfers between devices  135 us (48%)
  matrix products  60.9 us (21%)
  starting transfers between devices  29.8 us (10%)
  local copies, waits for them, and re-layouts  26.8 us (9%)
  other arithmetic  16.5 us (6%)
  between operations  13.6 us (5%)
    reduce_scatter x1, waiting for transfers between devices, body(): lax.psum_scatter(partial_value.astype(jnp.bfloat16), 'head', scatter_dime...  66.4 us
    all_to_all x2, waiting for transfers between devices, body(): lax.all_to_all(outgoing, 'seq', 0, 0, tiled=True).reshape(slots, width)  55.3 us
    all_to_all x2, starting transfers between devices, body(): lax.all_to_all(outgoing, 'seq', 0, 0, tiled=True).reshape(slots, width)  16.7 us
    dot_general x1, matrix products, body(): jnp.dot(own_rows, w_out[done_cols], preferred_element_type=jnp.float32)  14.7 us
    dot_general x2, matrix products, body(): jnp.einsum('qhd,khd->hqk', incoming[:, :part].reshape(head_shape), incomi...  13.6 us
    all_to_all x1, waiting for transfers between devices, body(): returned_prev = lax.all_to_all(back, 'seq', 0, 0, tiled=True)  13.5 us
    dot_general x2, matrix products, body(): jnp.einsum('hqk,khd->qhd', weights, incoming[:, 2 * part:3 * part].reshap...  13.2 us
    reduce_sum x2, other arithmetic, body(): totals = jnp.sum(exp_scores, axis=-1)  12.3 us
  transfers between devices with their start and end apart: 5, of which 3 were waited for; matrix products, arithmetic and copies ran while one was open for 28% of the time, Pallas kernels for 0%

profile of v6, /device:TPU:1, one launch (start us, length us, event | category | flops | bytes accessed | tf_op | source)
XLA Modules:
  0.0 282.9 jit_solution(6545637926668512949)
XLA Ops:
  6.5 0.6 compare_reduce_fusion
  7.2 1.0 add_select_fusion
  8.6 0.7 broadcast_select_fusion
  9.4 6.0 %convolution_convert_fusion = bf16[768,3200]{1,0:T(8,128)(2,1)} fusion(bf16[512,1]{1,0:T(8,128)(2,1)S(1)} %copy.57, bf16[512,1024]{1,0:T(8,128)(2,1)S(1)} %slice-done.4, bf16[512,1024]{1,0:T(8,128)(2,1)S(1)} %slice-done.2, bf16[512,1024]{1,0:T(8,128)(2,1)S(1)} %slice-done, s32[512]{0:T(512)S(1)} %multiply_add_fusion), kind=kOutput, calls=%fused_computation.15 | convolution fusion | flops 2535817216 | bytes 8064000 | tf_op jit(solution)/shard_map/dot_general | solution.py:71
  15.4 8.8 %all-to-all-start.1 = ((bf16[32,24,3200]{2,1,0:T(8,128)(2,1)}), bf16[32,24,3200]{2,1,0:T(8,128)(2,1)}, u32[]{:S(2)}, u32[]{:S(2)}) async-start(bf16[32,24,3200]{2,1,0:T(8,128)(2,1)} %bitcast.36), calls=%async_computation.1 | async-start | bytes 9830400 | tf_op jit(solution)/shard_map/all_to_all | solution.py:114
  24.2 2.9 %convolution_convert_fusion.1 = bf16[768,1536]{1,0:T(8,128)(2,1)} fusion(bf16[512,512]{1,0:T(8,128)(2,1)S(1)} %slice-done.5, bf16[512,512]{1,0:T(8,128)(2,1)S(1)} %slice-done.3, bf16[512,512]{1,0:T(8,128)(2,1)S(1)} %slice-done.1, s32[512]{0:T(512)S(1)} %multiply_add_fusion), kind=kOutput, calls=%fused_computation.21 | convolution fusion | flops 1214251008 | bytes 3934208 | tf_op jit(solution)/shard_map/dot_general | solution.py:71
  27.1 55.3 %all-to-all-done.1 = bf16[32,24,3200]{2,1,0:T(8,128)(2,1)} async-done(((bf16[32,24,3200]{2,1,0:T(8,128)(2,1)}), bf16[32,24,3200]{2,1,0:T(8,128)(2,1)}, u32[]{:S(2)}, u32[]{:S(2)}) %all-to-all-start.1) | async-done | bytes 4915232 | tf_op jit(solution)/shard_map/all_to_all | solution.py:114
  82.4 7.9 %all-to-all-start = ((bf16[32,24,1536]{2,1,0:T(8,128)(2,1)}), bf16[32,24,1536]{2,1,0:T(8,128)(2,1)S(1)}, u32[]{:S(2)}, u32[]{:S(2)}) async-start(bf16[32,24,1536]{2,1,0:T(8,128)(2,1)} %bitcast.39), calls=%async_computation | async-start | bytes 4718592 | tf_op jit(solution)/shard_map/all_to_all | solution.py:114
  90.3 1.1 add_reduce_fusion
  91.4 4.7 %fusion.62 = (bf16[768,1024]{1,0:T(8,128)(2,1)}, bf16[768,1024]{1,0:T(8,128)(2,1)}, bf16[768,1024]{1,0:T(8,128)(2,1)}) fusion(bf16[768,3200]{1,0:T(8,128)(2,1)} %bitcast.5), kind=kLoop, calls=%fused_computation.81 | loop fusion | bytes 9437184 | tf_op jit(solution)/shard_map/slice | solution.py:132
  96.6 2.6 copy.38
  99.2 2.6 copy.39
  101.9 11.7 %fusion = (f32[8,768]{1,0:T(8,128)S(1)}, f32[8,768,768]{1,2,0:T(8,128)}) fusion(pred[768,768]{0,1:T(8,128)(4,1)S(1)} %fusion.27, bf16[768,8,128]{0,2,1:T(8,128)(2,1)} %bitcast.34, bf16[768,8,128]{0,2,1:T(8,128)(2,1)} %bitcast.35), kind=kOutput, calls=%fused_computation.2 | convolution fusion | flops 1222109184 | bytes 22634496 | tf_op jit(solution)/shard_map/qhd,khd->hqk/dot_general | solution.py:129
  113.5 10.2 %fusion.1 = f32[8,768]{1,0:T(8,128)S(1)} fusion(f32[8,768,768]{1,2,0:T(8,128)} %get-tuple-element.38, f32[8,768]{1,0:T(8,128)S(1)} %get-tuple-element.37, pred[768,768]{0,1:T(8,128)(4,1)S(1)} %fusion.27), kind=kLoop, calls=%fused_computation.3 | loop fusion | flops 18868224 | bytes 19513344 | tf_op jit(solution)/shard_map/reduce_sum | solution.py:138
  123.8 2.6 copy.37
  126.4 10.3 %fusion.25 = bf16[768,8,128]{0,2,1:T(8,128)(2,1)} fusion(bf16[768,8,128]{0,2,1:T(8,128)(2,1)} %bitcast.40, f32[8,768,768]{1,2,0:T(8,128)} %get-tuple-element.38, f32[8,768]{1,0:T(8,128)S(1)} %get-tuple-element.37, pred[768,768]{0,1:T(8,128)(4,1)S(1)} %fusion.27, f32[768,8]{0,1:T(8,128)S(1)} %bitcast.43), kind=kOutput, calls=%fused_computation.31 | convolution fusion | flops 1228406784 | bytes 22659072 | tf_op jit(solution)/shard_map/hqk,khd->qhd/dot_general | solution.py:140
  136.6 2.9 %copy.43 = bf16[768,8,128]{2,1,0:T(8,128)(2,1)} copy(bf16[768,8,128]{0,2,1:T(8,128)(2,1)} %fusion.25) | data formatting | bytes 3145728 | tf_op jit(solution)/shard_map/convert_element_type | solution.py:147
  139.6 3.7 %reshape.289 = bf16[32,24,1024]{2,1,0:T(8,128)(2,1)} reshape(bf16[768,8,128]{2,1,0:T(8,128)(2,1)} %copy.43) | data formatting | bytes 3145728 | tf_op jit(solution)/shard_map/reshape | solution.py:147
  143.3 1.5 fusion.63
  144.7 1.4 copy.45
  146.1 1.4 copy.46
  147.5 1.4 copy.44
  148.9 7.5 %all-to-all-start.2 = ((bf16[32,24,1024]{2,1,0:T(8,128)(2,1)}), bf16[32,24,1024]{2,1,0:T(8,128)(2,1)}, u32[]{:S(2)}, u32[]{:S(2)}) async-start(bf16[32,24,1024]{2,1,0:T(8,128)(2,1)} %reshape.289), calls=%async_computation.2 | async-start | bytes 3145728 | tf_op jit(solution)/shard_map/all_to_all | solution.py:125
  156.5 1.9 fusion.8
  158.4 2.0 fusion.9
  160.5 3.0 %fusion.36 = bf16[768,4,128]{0,2,1:T(8,128)(2,1)S(1)} fusion(bf16[768,4,128]{0,2,1:T(8,128)(2,1)S(1)} %bitcast.41, f32[4,768,768]{1,2,0:T(8,128)S(1)} %get-tuple-element.40, f32[4,768]{1,0:T(4,128)S(1)} %get-tuple-element.39, pred[768,768]{0,1:T(8,128)(4,1)S(1)} %fusion.27, f32[768,4]{0,1:T(4,128)S(1)} %bitcast.44), kind=kOutput, calls=%fused_computation.43 | convolution fusion | flops 614203392 | bytes 11624448 | tf_op jit(solution)/shard_map/hqk,khd->qhd/dot_general | solution.py:140
  164.0 1.2 reshape.293
  165.2 13.5 %all-to-all-done.2 = bf16[32,24,1024]{2,1,0:T(8,128)(2,1)} async-done(((bf16[32,24,1024]{2,1,0:T(8,128)(2,1)}), bf16[32,24,1024]{2,1,0:T(8,128)(2,1)}, u32[]{:S(2)}, u32[]{:S(2)}) %all-to-all-start.2) | async-done | bytes 1572896 | tf_op jit(solution)/shard_map/all_to_all | solution.py:125
  178.7 5.5 %all-to-all-start.3 = ((bf16[32,24,512]{2,1,0:T(8,128)(2,1)}), bf16[32,24,512]{2,1,0:T(8,128)(2,1)S(1)}, u32[]{:S(2)}, u32[]{:S(2)}) async-start(bf16[32,24,512]{2,1,0:T(8,128)(2,1)} %reshape.293), calls=%async_computation.3 | async-start | bytes 1572864 | tf_op jit(solution)/shard_map/all_to_all | solution.py:154
  184.3 14.7 %fusion.3 = f32[512,6144]{1,0:T(8,128)} fusion(bf16[1536,6144]{1,0:T(8,128)(2,1)} %param.11, bf16[768,1024]{1,0:T(8,128)(2,1)} %bitcast.16, s32[512]{0:T(512)S(1)} %multiply_add_fusion), kind=kOutput, calls=%fused_computation.6 | convolution fusion | flops 7248674816 | bytes 26740736 | tf_op jit(solution)/shard_map/dot_general | solution.py:151
  199.0 10.6 %add_convert_fusion = bf16[512,6144]{1,0:T(8,128)(2,1)} fusion(f32[512,6144]{1,0:T(8,128)} %fusion.3, bf16[1536,6144]{1,0:T(8,128)(2,1)} %param.11, bf16[768,512]{1,0:T(8,128)(2,1)S(1)} %bitcast.42, s32[512]{0:T(512)S(1)} %multiply_add_fusion), kind=kOutput, calls=%fused_computation.5 | convolution fusion | flops 3630825472 | bytes 25954304 | tf_op jit(solution)/shard_map/dot_general | solution.py:158
  209.6 66.4 %reduce-scatter.2.cloned.1.call-done = bf16[512,1536]{1,0:T(8,128)(2,1)} async-done(((bf16[512,6144]{1,0:T(8,128)(2,1)}), bf16[512,1536]{1,0:T(8,128)(2,1)}) %reduce-scatter.2.cloned.1.call-update) | async-done | bytes 1572880 | tf_op jit(solution)/shard_map/reduce_scatter | solution.py:160
  (24 shorter events, 1.7 us)
Async XLA Ops:
  6.5 2.0 copy-start
  6.5 2.9 %slice-start = ((bf16[512,1536]{1,0:T(8,128)(2,1)}), bf16[512,1024]{1,0:T(8,128)(2,1)S(1)}, s32[]{:S(2)}) async-start(bf16[512,1536]{1,0:T(8,128)(2,1)} %param.7), calls=%async_computation.6 | async-start | bytes 2097152 | tf_op jit(solution)/shard_map/slice | solution.py:110
  6.5 2.9 %slice-start.2 = ((bf16[512,1536]{1,0:T(8,128)(2,1)}), bf16[512,1024]{1,0:T(8,128)(2,1)S(1)}, s32[]{:S(2)}) async-start(bf16[512,1536]{1,0:T(8,128)(2,1)} %param.8), calls=%async_computation.8 | async-start | bytes 2097152 | tf_op jit(solution)/shard_map/slice | solution.py:110
  6.5 2.9 %slice-start.4 = ((bf16[512,1536]{1,0:T(8,128)(2,1)}), bf16[512,1024]{1,0:T(8,128)(2,1)S(1)}, s32[]{:S(2)}) async-start(bf16[512,1536]{1,0:T(8,128)(2,1)} %param.9), calls=%async_computation.10 | async-start | bytes 2097152 | tf_op jit(solution)/shard_map/slice | solution.py:110
  15.4 8.8 %slice-start.1 = ((bf16[512,1536]{1,0:T(8,128)(2,1)}), bf16[512,512]{1,0:T(8,128)(2,1)S(1)}, s32[]{:S(2)}) async-start(bf16[512,1536]{1,0:T(8,128)(2,1)} %param.7), calls=%async_computation.7 | async-start | bytes 1048576 | tf_op jit(solution)/shard_map/slice | solution.py:110
  15.4 8.8 %slice-start.3 = ((bf16[512,1536]{1,0:T(8,128)(2,1)}), bf16[512,512]{1,0:T(8,128)(2,1)S(1)}, s32[]{:S(2)}) async-start(bf16[512,1536]{1,0:T(8,128)(2,1)} %param.8), calls=%async_computation.9 | async-start | bytes 1048576 | tf_op jit(solution)/shard_map/slice | solution.py:110
  15.4 8.8 %slice-start.5 = ((bf16[512,1536]{1,0:T(8,128)(2,1)}), bf16[512,512]{1,0:T(8,128)(2,1)S(1)}, s32[]{:S(2)}) async-start(bf16[512,1536]{1,0:T(8,128)(2,1)} %param.9), calls=%async_computation.11 | async-start | bytes 1048576 | tf_op jit(solution)/shard_map/slice | solution.py:110
  15.4 67.0 %all-to-all-start.1 = ((bf16[32,24,3200]{2,1,0:T(8,128)(2,1)}), bf16[32,24,3200]{2,1,0:T(8,128)(2,1)}, u32[]{:S(2)}, u32[]{:S(2)}) async-start(bf16[32,24,3200]{2,1,0:T(8,128)(2,1)} %bitcast.36), calls=%async_computation.1 | async-start | bytes 9830400 | tf_op jit(solution)/shard_map/all_to_all | solution.py:114
  82.4 60.9 %all-to-all-start = ((bf16[32,24,1536]{2,1,0:T(8,128)(2,1)}), bf16[32,24,1536]{2,1,0:T(8,128)(2,1)S(1)}, u32[]{:S(2)}, u32[]{:S(2)}) async-start(bf16[32,24,1536]{2,1,0:T(8,128)(2,1)} %bitcast.39), calls=%async_computation | async-start | bytes 4718592 | tf_op jit(solution)/shard_map/all_to_all | solution.py:114
  148.9 29.8 %all-to-all-start.2 = ((bf16[32,24,1024]{2,1,0:T(8,128)(2,1)}), bf16[32,24,1024]{2,1,0:T(8,128)(2,1)}, u32[]{:S(2)}, u32[]{:S(2)}) async-start(bf16[32,24,1024]{2,1,0:T(8,128)(2,1)} %reshape.289), calls=%async_computation.2 | async-start | bytes 3145728 | tf_op jit(solution)/shard_map/all_to_all | solution.py:125
  178.7 20.2 %all-to-all-start.3 = ((bf16[32,24,512]{2,1,0:T(8,128)(2,1)}), bf16[32,24,512]{2,1,0:T(8,128)(2,1)S(1)}, u32[]{:S(2)}, u32[]{:S(2)}) async-start(bf16[32,24,512]{2,1,0:T(8,128)(2,1)} %reshape.293), calls=%async_computation.3 | async-start | bytes 1572864 | tf_op jit(solution)/shard_map/all_to_all | solution.py:154
  184.3 91.7 %reduce-scatter.2.cloned.1.call-start = ((), (), s32[]{:S(2)}) async-start(), calls=%async_computation.5 | async-start | bytes 7864320 | tf_op jit(solution)/shard_map/reduce_scatter | solution.py:160
Sparse Core Ops, SparseCore 0:
  209.7 66.2 reduce-scatter.1
